TPU v7x, 256 devices: a whole 4x4x8 slice. The times are simulated.
256 devices in a mesh: sec: 2 (over z_hi), lat: 4 (over x), lon: 32 (over y, z_lo, core).
Axes of the slice: x: 4, y: 4, z: 8 (z_hi: 2, z_lo: 4; z = z_hi * 4 + z_lo), core: 2. Of those that a mesh axis runs over, the one named last changes fastest.
Arguments:
- spectra: float32 [36, 36, 32, 4096], P('sec', None, 'lat', 'lon'), may hold values from 0 to 2
- currents: float32 [2, 8, 32, 4096], P(None, 'sec', 'lat', 'lon'), may hold values from -3 to 3
- land_mask: int32 [32, 4096], P('lat', 'lon'), may hold values 0 or 1
- diffusion: float32 [32, 4096], P('lat', 'lon'), may hold values from 0.08 to 0.19
- courant: float32 [36], P('sec'), may hold values from 0.15 to 0.45
- stokes_weight: float32 [36], P('sec'), may hold values from 0.02 to 0.1
- stress_weight: float32 [36], P('sec'), may hold values from 0.02 to 0.1
Outputs:
- new_spectra: float32 [36, 36, 32, 4096], P('sec', None, 'lat', 'lon')
- new_currents: float32 [2, 8, 32, 4096], P(None, 'sec', 'lat', 'lon')
Inputs may be any that keep to these rules, and one draw needn't show every extreme that they name: `land_mask`: 1 marks a sea column, 0 a land column.
All inputs are finite; a program needn't handle non-finite values. No bound on the sum of `land_mask` on one device may be relied on, other than what follows from the above.
Results may differ from a plain program's by a relative error of at most 0.0001.
Values sent between devices are 32-bit elements; how exact they have to be, the bound alone decides.
A program may use at most 128 MiB of HBM per device.

v0:
```python
import math

import jax
import jax.numpy as jnp
from jax import lax
from jax.sharding import PartitionSpec as P

ITERS = 4


current_gain = 0.1
stress_gain = 0.5


def broadcast(array, axis, root):
    mine = lax.axis_index(axis) == root
    return lax.psum(jnp.where(mine, array, jnp.zeros_like(array)), axis)


def padded_2(block, sides, width):
    for axis, dim in sides:
        count = lax.axis_size(axis)
        forward = [(i, i + 1) for i in range(count - 1)]
        forward.append((count - 1, 0))
        backward = [(target, source) for source, target in forward]
        low = lax.ppermute(
            lax.slice_in_dim(block, block.shape[dim] - width, None, axis=dim), axis, forward
        )
        high = lax.ppermute(lax.slice_in_dim(block, 0, width, axis=dim), axis, backward)
        block = jnp.concatenate([low, block, high], axis=dim)
    return block


def heading_tables(directions):
    heading = (jnp.arange(directions).astype(jnp.float32) + 0.5) * (2.0 * math.pi / directions)
    return (jnp.cos(heading), jnp.sin(heading))


def wave_update(
    energy,
    west_cell,
    east_cell,
    south_cell,
    north_cell,
    speed,
    cosine_table,
    sine_table,
    surface,
    sea_cells,
):
    speed_x = (speed[:, None] * cosine_table[None])[:, :, None, None]
    speed_y = (speed[:, None] * sine_table[None])[:, :, None, None]
    step_x = jnp.maximum(speed_x, 0.0) * (energy - west_cell) + jnp.minimum(speed_x, 0.0) * (
        east_cell - energy
    )
    step_y = jnp.maximum(speed_y, 0.0) * (energy - south_cell) + jnp.minimum(speed_y, 0.0) * (
        north_cell - energy
    )
    advected = energy - step_x - step_y
    doppler = 1.0 + current_gain * (
        surface[0][None] * cosine_table[:, None, None]
        + surface[1][None] * sine_table[:, None, None]
    )
    return sea_cells * (advected * doppler)


def coupling_weights(stokes_w, stress_w, cosine_table, sine_table):
    stacked = jnp.stack(
        [
            stokes_w[:, None] * cosine_table[None],
            stokes_w[:, None] * sine_table[None],
            stress_w[:, None] * cosine_table[None],
            stress_w[:, None] * sine_table[None],
        ]
    )
    return stacked.reshape(4, stokes_w.shape[0] * cosine_table.shape[0])


def vertical_rate(level):
    return 0.04 + 0.0125 * (7 * level % 5).astype(jnp.float32)


def coriolis_rate(row_index, total_rows):
    return 0.05 + 0.1 * (row_index.astype(jnp.float32) + 0.5) / total_rows


def valid_rows(first_row, row_count, total_rows):
    row_index = first_row + jnp.arange(row_count)
    return ((row_index >= 0) & (row_index < total_rows)).astype(jnp.float32)


def ocean_step(extended, column_data, first_level, first_row, total_levels, total_rows):
    center = extended[:, 1:-1, 1:-1, 1:-1]
    laplace = (
        extended[:, 1:-1, 2:, 1:-1]
        + extended[:, 1:-1, :-2, 1:-1]
        + extended[:, 1:-1, 1:-1, 2:]
        + extended[:, 1:-1, 1:-1, :-2]
        - 4.0 * center
    )
    level_above = extended[:, :-2, 1:-1, 1:-1]
    level_below = extended[:, 2:, 1:-1, 1:-1]
    level = first_level + 1 + jnp.arange(center.shape[1])
    has_up = (level > 0)[:, None, None]
    has_down = (level < total_levels - 1)[:, None, None]
    mixing = vertical_rate(level)[:, None, None]
    vertical = mixing * (
        jnp.where(has_up, level_above - center, 0.0)
        + jnp.where(has_down, level_below - center, 0.0)
    )
    stokes_decay = (1.0 / (1.0 + level.astype(jnp.float32)))[:, None, None]
    top_gain = jnp.where(level == 0, stress_gain, 0.0)[:, None, None]
    row_index = first_row + 1 + jnp.arange(center.shape[2])
    coriolis = coriolis_rate(row_index, total_rows)[:, None]
    sea_cells = column_data[0]
    kappa = column_data[1]
    zonal = center[0]
    meridional = center[1]
    zonal_new = sea_cells * (
        zonal
        + kappa * laplace[0]
        + vertical[0]
        + coriolis * (meridional + stokes_decay * column_data[3])
        + top_gain * column_data[4]
    )
    meridional_new = sea_cells * (
        meridional
        + kappa * laplace[1]
        + vertical[1]
        - coriolis * (zonal + stokes_decay * column_data[2])
        + top_gain * column_data[5]
    )
    return jnp.stack([zonal_new, meridional_new])


def shards(spectra, currents, land_mask, diffusion, courant, stokes_weight, stress_weight):
    freq_dev, directions, tile_rows, tile_cols = spectra.shape
    levels = currents.shape[1]
    sec_count = lax.axis_size("sec")
    lat_count = lax.axis_size("lat")
    sec_index = lax.axis_index("sec")
    lat_index = lax.axis_index("lat")
    total_rows = tile_rows * lat_count
    total_levels = levels * sec_count
    level_base = sec_index * levels
    row_base = lat_index * tile_rows
    sea_cells = land_mask.astype(jnp.float32)
    cosine_table, sine_table = heading_tables(directions)
    surface = broadcast(currents[:, 0], "sec", 0)
    padded = padded_2(spectra, (("lat", 2), ("lon", 3)), 1)
    south_ok = (lat_index > 0).astype(jnp.float32)
    north_ok = (lat_index < lat_count - 1).astype(jnp.float32)
    west_cell = padded[:, :, 1:-1, :-2]
    east_cell = padded[:, :, 1:-1, 2:]
    south_rim = padded[:, :, :1, 1:-1] * south_ok
    north_rim = padded[:, :, -1:, 1:-1] * north_ok
    south_cell = jnp.concatenate([south_rim, spectra[:, :, :-1]], axis=2)
    north_cell = jnp.concatenate([spectra[:, :, 1:], north_rim], axis=2)
    new_spectra = wave_update(
        spectra,
        west_cell,
        east_cell,
        south_cell,
        north_cell,
        courant,
        cosine_table,
        sine_table,
        surface,
        sea_cells,
    )
    weights = coupling_weights(stokes_weight, stress_weight, cosine_table, sine_table)
    partial_value = jnp.dot(
        weights,
        new_spectra.reshape(freq_dev * directions, tile_rows * tile_cols),
        precision=lax.Precision.HIGHEST,
        preferred_element_type=jnp.float32,
    )
    coupling = lax.psum(partial_value, "sec").reshape(4, tile_rows, tile_cols)
    column_data = jnp.concatenate([sea_cells[None], diffusion[None], coupling], axis=0)
    fields = currents * sea_cells
    row_ok = valid_rows(row_base - 1, tile_rows + 2, total_rows)[:, None]
    for iteration in range(ITERS):
        extended = padded_2(fields, (("sec", 1), ("lat", 2), ("lon", 3)), 1)
        extended = extended * row_ok
        fields = ocean_step(
            extended, column_data, level_base - 1, row_base - 1, total_levels, total_rows
        )
    return (new_spectra, fields)


def solution(mesh):
    in_specs = (
        P("sec", None, "lat", "lon"),
        P(None, "sec", "lat", "lon"),
        P("lat", "lon"),
        P("lat", "lon"),
        P("sec"),
        P("sec"),
        P("sec"),
    )
    out_specs = (P("sec", None, "lat", "lon"), P(None, "sec", "lat", "lon"))
    return jax.shard_map(shards, mesh=mesh, in_specs=in_specs, out_specs=out_specs, check_vma=False)
```

profile of v0, /device:TPU:1, one launch (start us, length us, event | category | flops | bytes accessed | tf_op | source)
XLA Modules:
  0.0 199.7 jit_solution(15489876281411188037)
XLA Ops:
  0.6 3.2 %fusion.84 = (f32[18,36,1,128]{3,2,1,0:T(1,128)S(1)}, f32[18,36,1,128]{3,2,1,0:T(1,128)S(1)}) fusion(f32[18,36,8,128]{3,2,1,0:T(8,128)} %param.7), kind=kLoop, calls=%fused_computation.189 | loop fusion | bytes 1327104 | tf_op jit(solution)/shard_map/slice | solution.py:27
  4.6 3.3 %collective-permute-start.1 = (f32[18,36,1,128]{3,1,2,0:T(8,128)}, f32[18,36,1,128]{3,1,2,0:T(8,128)S(1)}, u32[]{:S(2)}, u32[]{:S(2)}) collective-permute-start(f32[18,36,1,128]{3,1,2,0:T(8,128)} %copy.82), channel_id=1, source_target_pairs={{32,0},{64,32},{96,64},{0,96},{33,1},{65,33},{97,65},{1,97},{34,2}... | collective-permute-start | bytes 995336 | tf_op jit(solution)/shard_map/ppermute | solution.py:29
  10.7 6.9 %collective-permute-start.5 = (f32[2,1,8,128]{3,2,1,0:T(8,128)S(1)}, f32[2,1,8,128]{3,2,1,0:T(8,128)S(1)}, u32[]{:S(2)}, u32[]{:S(2)}) collective-permute-start(f32[2,1,8,128]{3,2,1,0:T(8,128)S(1)} %get-tuple-element.55), channel_id=1, source_target_pairs={{128,0},{0,128},{129,1},{1,129},{130,2},{2,130},{131,3},{3,131},{1... | collective-permute-start | bytes 24584 | tf_op jit(solution)/shard_map/ppermute | solution.py:29
  17.7 2.9 %fusion.83 = (f32[18,36,7,128]{3,2,1,0:T(8,128)}, f32[18,36,7,128]{3,2,1,0:T(8,128)}) fusion(f32[18,36,8,128]{3,2,1,0:T(8,128)S(1)} %copy-done.1), kind=kLoop, calls=%fused_computation.188 | loop fusion | bytes 9289728 | tf_op jit(solution)/shard_map/slice | solution.py:158
  23.2 7.7 %psum.14 = f32[2,8,128]{2,1,0:T(8,128)S(1)} all-reduce(f32[2,8,128]{2,1,0:T(8,128)S(1)} %select_bitcast_fusion), channel_id=1, replica_groups=mesh['sec'=2,'lat'=4,'lon'=32] {'sec'}, use_global_device_ids=true, to_apply=%region_0.1 | all-reduce | flops 2048 | bytes 16384 | tf_op jit(solution)/shard_map/psum | solution.py:17
  34.0 2.8 %collective-permute-start.7 = (f32[2,6,1,128]{3,2,1,0:T(1,128)S(1)}, f32[2,6,1,128]{3,2,1,0:T(1,128)S(1)}, u32[]{:S(2)}, u32[]{:S(2)}) collective-permute-start(f32[2,6,1,128]{3,2,1,0:T(1,128)S(1)} %get-tuple-element.47), channel_id=1, source_target_pairs={{32,0},{64,32},{96,64},{0,96},{33,1},{65,33},{97,65},{1,97},{34,2}... | collective-permute-start | bytes 18440 | tf_op jit(solution)/shard_map/ppermute | solution.py:29
  37.4 7.3 %copy.61 = f32[18,36,8,128]{1,0,3,2:T(8,128)} copy(f32[18,36,8,128]{3,2,1,0:T(8,128)S(1)} %copy-done.1) | data formatting | bytes 5308416 | tf_op args[0]
  45.4 2.9 %collective-permute-start.9 = (f32[2,6,10,1]{3,2,1,0:T(8,128)}, f32[2,6,10,1]{3,2,1,0:T(8,128)S(1)}, u32[]{:S(2)}, u32[]{:S(2)}) collective-permute-start(f32[2,6,10,1]{3,2,1,0:T(8,128)} %get-tuple-element.39), channel_id=1, source_target_pairs={{1,0},{2,1},{3,2},{4,3},{5,4},{6,5},{7,6},{8,7},{9,8},{10,9},{11,1... | collective-permute-start | bytes 1448 | tf_op jit(solution)/shard_map/ppermute | solution.py:29
  49.1 3.6 %copy.84 = f32[18,36,7,128]{3,1,2,0:T(8,128)} copy(f32[18,36,7,128]{3,2,1,0:T(8,128)} %get-tuple-element.13) | data formatting | bytes 4644864
  52.7 3.7 %copy.85 = f32[18,36,7,128]{3,1,2,0:T(8,128)} copy(f32[18,36,7,128]{3,2,1,0:T(8,128)} %get-tuple-element.12) | data formatting | bytes 4644864
  59.7 1.6 copy.62
  61.3 1.6 copy.60
  63.0 6.2 %pad_maximum_fusion = f32[18,36,10,128]{1,0,3,2:T(8,128)S(1)} fusion(f32[18,36,1,128]{1,0,3,2:T(8,128)} %copy.62, f32[18,36,8,128]{1,0,3,2:T(8,128)} %copy.61, f32[18,36,1,128]{1,0,3,2:T(8,128)} %copy.60), kind=kLoop, calls=%fused_computation | loop fusion | flops 1658880 | bytes 6635520 | tf_op jit(solution)/shard_map/concatenate | solution.py:30
  69.2 5.4 %copy-done = f32[18,36,10,128]{1,0,3,2:T(8,128)} copy-done((f32[18,36,10,128]{1,0,3,2:T(8,128)}, f32[18,36,10,128]{1,0,3,2:T(8,128)S(1)}, u32[]{:S(2)}) %copy-start) | copy-done | bytes 3317784
  75.3 2.8 %collective-permute-start.3 = (f32[18,36,10,1]{1,0,3,2:T(8,128)}, f32[18,36,10,1]{1,0,3,2:T(8,128)}, u32[]{:S(2)}, u32[]{:S(2)}) collective-permute-start(f32[18,36,10,1]{1,0,3,2:T(8,128)} %get-tuple-element.11), channel_id=1, source_target_pairs={{1,0},{2,1},{3,2},{4,3},{5,4},{6,5},{7,6},{8,7},{9,8},{10,9},{11,1... | collective-permute-start | bytes 77768 | tf_op jit(solution)/shard_map/ppermute | solution.py:29
  78.9 11.9 %copy.64 = f32[18,36,10,128]{3,1,2,0:T(8,128)} copy(f32[18,36,10,128]{1,0,3,2:T(8,128)} %copy-done) | data formatting | bytes 6635520 | tf_op jit(solution)/shard_map/concatenate | solution.py:30
  90.8 3.6 %copy.67 = f32[18,36,10,1]{3,1,2,0:T(8,128)} copy(f32[18,36,10,1]{1,0,3,2:T(8,128)} %collective-permute-done.3) | data formatting | bytes 51840 | tf_op jit(solution)/shard_map/ppermute | solution.py:29
  94.4 3.6 %copy.63 = f32[18,36,10,1]{3,1,2,0:T(8,128)} copy(f32[18,36,10,1]{1,0,3,2:T(8,128)} %collective-permute-done.2) | data formatting | bytes 51840 | tf_op jit(solution)/shard_map/ppermute | solution.py:26
  98.0 7.7 %fusion.6 = f32[18,36,8,128]{3,1,2,0:T(8,128)S(1)} fusion(f32[18,36,10,1]{3,1,2,0:T(8,128)} %copy.67, f32[18,36,10,128]{3,1,2,0:T(8,128)} %copy.64, f32[18,36,10,1]{3,1,2,0:T(8,128)} %copy.63, f32[18,36,7,128]{3,1,2,0:T(8,128)} %copy.84, f32[18,36,1,128]{3,1,2,0:T(8,128)S(1)} %copy-done.3, f32[18,36,1,128]{3,1,2,0:T(8,128)S(1)} %broadcast_multiply_fusion, ...), kind=kLoop, calls=%fused_computation.8 | loop fusion | flops 11943936 | bytes 14148352 | tf_op jit(solution)/shard_map/mul | solution.py:64
  106.4 1.7 fusion.12
  108.1 13.3 %psum.15 = f32[4,1024]{1,0:T(4,128)S(1)} all-reduce(f32[4,1024]{1,0:T(4,128)S(1)} %fusion.12), channel_id=1, replica_groups=mesh['sec'=2,'lat'=4,'lon'=32] {'sec'}, use_global_device_ids=true, to_apply=%region_1.2 | all-reduce | flops 4096 | bytes 32768 | tf_op jit(solution)/shard_map/psum | solution.py:178
  123.4 4.5 %collective-permute-start.10 = (f32[2,1,8,128]{3,2,1,0:T(8,128)S(1)}, f32[2,1,8,128]{3,2,1,0:T(8,128)S(1)}, u32[]{:S(2)}, u32[]{:S(2)}) collective-permute-start(f32[2,1,8,128]{3,2,1,0:T(8,128)S(1)} %get-tuple-element.52), channel_id=1, source_target_pairs={{0,128},{128,0},{1,129},{129,1},{2,130},{130,2},{3,131},{131,3},{4... | collective-permute-start | bytes 24584 | tf_op jit(solution)/shard_map/ppermute | solution.py:26
  129.9 2.8 %collective-permute-start.13 = (f32[2,6,1,128]{3,2,1,0:T(1,128)S(1)}, f32[2,6,1,128]{3,2,1,0:T(1,128)S(1)}, u32[]{:S(2)}, u32[]{:S(2)}) collective-permute-start(f32[2,6,1,128]{3,2,1,0:T(1,128)S(1)} %get-tuple-element.45), channel_id=1, source_target_pairs={{32,0},{64,32},{96,64},{0,96},{33,1},{65,33},{97,65},{1,97},{34,2}... | collective-permute-start | bytes 18440 | tf_op jit(solution)/shard_map/ppermute | solution.py:29
  133.4 3.2 %collective-permute-done.12 = f32[2,6,1,128]{3,2,1,0:T(1,128)S(1)} collective-permute-done((f32[2,6,1,128]{3,2,1,0:T(1,128)S(1)}, f32[2,6,1,128]{3,2,1,0:T(1,128)S(1)}, u32[]{:S(2)}, u32[]{:S(2)}) %collective-permute-start.12) | collective-permute-done | bytes 6176 | tf_op jit(solution)/shard_map/ppermute | solution.py:26
  136.7 9.4 %collective-permute-start.15 = (f32[2,6,10,1]{3,2,1,0:T(8,128)S(1)}, f32[2,6,10,1]{3,2,1,0:T(8,128)S(1)}, u32[]{:S(2)}, u32[]{:S(2)}) collective-permute-start(f32[2,6,10,1]{3,2,1,0:T(8,128)S(1)} %get-tuple-element.37), channel_id=1, source_target_pairs={{1,0},{2,1},{3,2},{4,3},{5,4},{6,5},{7,6},{8,7},{9,8},{10,9},{11,1... | collective-permute-start | bytes 1448 | tf_op jit(solution)/shard_map/ppermute | solution.py:29
  148.3 4.3 %collective-permute-start.17 = (f32[2,1,8,128]{3,2,1,0:T(8,128)S(1)}, f32[2,1,8,128]{3,2,1,0:T(8,128)S(1)}, u32[]{:S(2)}, u32[]{:S(2)}) collective-permute-start(f32[2,1,8,128]{3,2,1,0:T(8,128)S(1)} %get-tuple-element.51), channel_id=1, source_target_pairs={{128,0},{0,128},{129,1},{1,129},{130,2},{2,130},{131,3},{3,131},{1... | collective-permute-start | bytes 24584 | tf_op jit(solution)/shard_map/ppermute | solution.py:29
  154.8 4.2 %collective-permute-done.16 = f32[2,1,8,128]{3,2,1,0:T(8,128)S(1)} collective-permute-done((f32[2,1,8,128]{3,2,1,0:T(8,128)S(1)}, f32[2,1,8,128]{3,2,1,0:T(8,128)S(1)}, u32[]{:S(2)}, u32[]{:S(2)}) %collective-permute-start.16) | collective-permute-done | bytes 8224 | tf_op jit(solution)/shard_map/ppermute | solution.py:26
  163.2 10.2 %collective-permute-start.21 = (f32[2,6,10,1]{3,2,1,0:T(8,128)S(1)}, f32[2,6,10,1]{3,2,1,0:T(8,128)S(1)}, u32[]{:S(2)}, u32[]{:S(2)}) collective-permute-start(f32[2,6,10,1]{3,2,1,0:T(8,128)S(1)} %get-tuple-element.35), channel_id=1, source_target_pairs={{1,0},{2,1},{3,2},{4,3},{5,4},{6,5},{7,6},{8,7},{9,8},{10,9},{11,1... | collective-permute-start | bytes 1448 | tf_op jit(solution)/shard_map/ppermute | solution.py:29
  174.3 1.5 collective-permute-done.20
  177.4 4.3 %collective-permute-start.22 = (f32[2,1,8,128]{3,2,1,0:T(8,128)S(1)}, f32[2,1,8,128]{3,2,1,0:T(8,128)S(1)}, u32[]{:S(2)}, u32[]{:S(2)}) collective-permute-start(f32[2,1,8,128]{3,2,1,0:T(8,128)S(1)} %get-tuple-element.48), channel_id=1, source_target_pairs={{0,128},{128,0},{1,129},{129,1},{2,130},{130,2},{3,131},{131,3},{4... | collective-permute-start | bytes 24584 | tf_op jit(solution)/shard_map/ppermute | solution.py:26
  186.4 1.6 collective-permute-done.24
  188.1 8.1 %collective-permute-start.27 = (f32[2,6,10,1]{3,2,1,0:T(8,128)S(1)}, f32[2,6,10,1]{3,2,1,0:T(8,128)S(1)}, u32[]{:S(2)}, u32[]{:S(2)}) collective-permute-start(f32[2,6,10,1]{3,2,1,0:T(8,128)S(1)} %get-tuple-element.33), channel_id=1, source_target_pairs={{1,0},{2,1},{3,2},{4,3},{5,4},{6,5},{7,6},{8,7},{9,8},{10,9},{11,1... | collective-permute-start | bytes 1448 | tf_op jit(solution)/shard_map/ppermute | solution.py:29
  (146 shorter events, 40.7 us)
Async XLA Ops:
  4.6 55.1 %collective-permute-start.1 = (f32[18,36,1,128]{3,1,2,0:T(8,128)}, f32[18,36,1,128]{3,1,2,0:T(8,128)S(1)}, u32[]{:S(2)}, u32[]{:S(2)}) collective-permute-start(f32[18,36,1,128]{3,1,2,0:T(8,128)} %copy.82), channel_id=1, source_target_pairs={{32,0},{64,32},{96,64},{0,96},{33,1},{65,33},{97,65},{1,97},{34,2}... | collective-permute-start | bytes 995336 | tf_op jit(solution)/shard_map/ppermute | solution.py:29
  8.6 52.7 %collective-permute-start = (f32[18,36,1,128]{3,1,2,0:T(8,128)}, f32[18,36,1,128]{3,1,2,0:T(8,128)S(1)}, u32[]{:S(2)}, u32[]{:S(2)}) collective-permute-start(f32[18,36,1,128]{3,1,2,0:T(8,128)} %copy.83), channel_id=1, source_target_pairs={{0,32},{32,64},{64,96},{96,0},{1,33},{33,65},{65,97},{97,1},{2,34}... | collective-permute-start | bytes 995336 | tf_op jit(solution)/shard_map/ppermute | solution.py:26
  10.7 23.3 %collective-permute-start.5 = (f32[2,1,8,128]{3,2,1,0:T(8,128)S(1)}, f32[2,1,8,128]{3,2,1,0:T(8,128)S(1)}, u32[]{:S(2)}, u32[]{:S(2)}) collective-permute-start(f32[2,1,8,128]{3,2,1,0:T(8,128)S(1)} %get-tuple-element.55), channel_id=1, source_target_pairs={{128,0},{0,128},{129,1},{1,129},{130,2},{2,130},{131,3},{3,131},{1... | collective-permute-start | bytes 24584 | tf_op jit(solution)/shard_map/ppermute | solution.py:29
  17.6 16.4 %collective-permute-start.4 = (f32[2,1,8,128]{3,2,1,0:T(8,128)S(1)}, f32[2,1,8,128]{3,2,1,0:T(8,128)S(1)}, u32[]{:S(2)}, u32[]{:S(2)}) collective-permute-start(f32[2,1,8,128]{3,2,1,0:T(8,128)S(1)} %get-tuple-element.54), channel_id=1, source_target_pairs={{0,128},{128,0},{1,129},{129,1},{2,130},{130,2},{3,131},{131,3},{4... | collective-permute-start | bytes 24584 | tf_op jit(solution)/shard_map/ppermute | solution.py:26
  34.0 10.6 %collective-permute-start.7 = (f32[2,6,1,128]{3,2,1,0:T(1,128)S(1)}, f32[2,6,1,128]{3,2,1,0:T(1,128)S(1)}, u32[]{:S(2)}, u32[]{:S(2)}) collective-permute-start(f32[2,6,1,128]{3,2,1,0:T(1,128)S(1)} %get-tuple-element.47), channel_id=1, source_target_pairs={{32,0},{64,32},{96,64},{0,96},{33,1},{65,33},{97,65},{1,97},{34,2}... | collective-permute-start | bytes 18440 | tf_op jit(solution)/shard_map/ppermute | solution.py:29
  36.8 7.9 %collective-permute-start.6 = (f32[2,6,1,128]{3,2,1,0:T(1,128)S(1)}, f32[2,6,1,128]{3,2,1,0:T(1,128)S(1)}, u32[]{:S(2)}, u32[]{:S(2)}) collective-permute-start(f32[2,6,1,128]{3,2,1,0:T(1,128)S(1)} %get-tuple-element.46), channel_id=1, source_target_pairs={{0,32},{32,64},{64,96},{96,0},{1,33},{33,65},{65,97},{97,1},{2,34}... | collective-permute-start | bytes 18440 | tf_op jit(solution)/shard_map/ppermute | solution.py:26
  45.4 11.0 %collective-permute-start.9 = (f32[2,6,10,1]{3,2,1,0:T(8,128)}, f32[2,6,10,1]{3,2,1,0:T(8,128)S(1)}, u32[]{:S(2)}, u32[]{:S(2)}) collective-permute-start(f32[2,6,10,1]{3,2,1,0:T(8,128)} %get-tuple-element.39), channel_id=1, source_target_pairs={{1,0},{2,1},{3,2},{4,3},{5,4},{6,5},{7,6},{8,7},{9,8},{10,9},{11,1... | collective-permute-start | bytes 1448 | tf_op jit(solution)/shard_map/ppermute | solution.py:29
  48.4 8.1 %collective-permute-start.8 = (f32[2,6,10,1]{3,2,1,0:T(8,128)}, f32[2,6,10,1]{3,2,1,0:T(8,128)}, u32[]{:S(2)}, u32[]{:S(2)}) collective-permute-start(f32[2,6,10,1]{3,2,1,0:T(8,128)} %get-tuple-element.38), channel_id=1, source_target_pairs={{0,1},{1,2},{2,3},{3,4},{4,5},{5,6},{6,7},{7,8},{8,9},{9,10},{10,1... | collective-permute-start | bytes 1448 | tf_op jit(solution)/shard_map/ppermute | solution.py:26
  75.3 15.5 %collective-permute-start.3 = (f32[18,36,10,1]{1,0,3,2:T(8,128)}, f32[18,36,10,1]{1,0,3,2:T(8,128)}, u32[]{:S(2)}, u32[]{:S(2)}) collective-permute-start(f32[18,36,10,1]{1,0,3,2:T(8,128)} %get-tuple-element.11), channel_id=1, source_target_pairs={{1,0},{2,1},{3,2},{4,3},{5,4},{6,5},{7,6},{8,7},{9,8},{10,9},{11,1... | collective-permute-start | bytes 77768 | tf_op jit(solution)/shard_map/ppermute | solution.py:29
  78.1 16.3 %collective-permute-start.2 = (f32[18,36,10,1]{1,0,3,2:T(8,128)}, f32[18,36,10,1]{1,0,3,2:T(8,128)}, u32[]{:S(2)}, u32[]{:S(2)}) collective-permute-start(f32[18,36,10,1]{1,0,3,2:T(8,128)} %get-tuple-element.10), channel_id=1, source_target_pairs={{0,1},{1,2},{2,3},{3,4},{4,5},{5,6},{6,7},{7,8},{8,9},{9,10},{10,1... | collective-permute-start | bytes 77768 | tf_op jit(solution)/shard_map/ppermute | solution.py:26
  106.3 69.8 %copy-start.2 = (f32[18,36,8,128]{3,2,1,0:T(8,128)}, f32[18,36,8,128]{3,2,1,0:T(8,128)S(1)}, u32[]{:S(2)}) copy-start(f32[18,36,8,128]{3,2,1,0:T(8,128)S(1)} %copy.75) | copy-start | bytes 7962628
  106.3 41.7 %copy-start.17 = (pred[4]{0:T(512)(128)(4,1)S(1)}, pred[4]{0:T(512)(128)(4,1)}, u32[]{:S(2)}) copy-start(pred[4]{0:T(512)(128)(4,1)} %get-tuple-element.76) | copy-start | bytes 16
  106.3 41.7 %copy-start.18 = (pred[4]{0:T(512)(128)(4,1)S(1)}, pred[4]{0:T(512)(128)(4,1)}, u32[]{:S(2)}) copy-start(pred[4]{0:T(512)(128)(4,1)} %get-tuple-element.77) | copy-start | bytes 16
  106.3 41.7 %copy-start.19 = (f32[4]{0:T(128)S(1)}, f32[4]{0:T(128)}, u32[]{:S(2)}) copy-start(f32[4]{0:T(128)} %get-tuple-element.75) | copy-start | bytes 52
  122.5 6.5 %collective-permute-start.11 = (f32[2,1,8,128]{3,2,1,0:T(8,128)S(1)}, f32[2,1,8,128]{3,2,1,0:T(8,128)S(1)}, u32[]{:S(2)}, u32[]{:S(2)}) collective-permute-start(f32[2,1,8,128]{3,2,1,0:T(8,128)S(1)} %get-tuple-element.53), channel_id=1, source_target_pairs={{128,0},{0,128},{129,1},{1,129},{130,2},{2,130},{131,3},{3,131},{1... | collective-permute-start | bytes 24584 | tf_op jit(solution)/shard_map/ppermute | solution.py:29
  123.4 6.4 %collective-permute-start.10 = (f32[2,1,8,128]{3,2,1,0:T(8,128)S(1)}, f32[2,1,8,128]{3,2,1,0:T(8,128)S(1)}, u32[]{:S(2)}, u32[]{:S(2)}) collective-permute-start(f32[2,1,8,128]{3,2,1,0:T(8,128)S(1)} %get-tuple-element.52), channel_id=1, source_target_pairs={{0,128},{128,0},{1,129},{129,1},{2,130},{130,2},{3,131},{131,3},{4... | collective-permute-start | bytes 24584 | tf_op jit(solution)/shard_map/ppermute | solution.py:26
  129.9 3.5 %collective-permute-start.13 = (f32[2,6,1,128]{3,2,1,0:T(1,128)S(1)}, f32[2,6,1,128]{3,2,1,0:T(1,128)S(1)}, u32[]{:S(2)}, u32[]{:S(2)}) collective-permute-start(f32[2,6,1,128]{3,2,1,0:T(1,128)S(1)} %get-tuple-element.45), channel_id=1, source_target_pairs={{32,0},{64,32},{96,64},{0,96},{33,1},{65,33},{97,65},{1,97},{34,2}... | collective-permute-start | bytes 18440 | tf_op jit(solution)/shard_map/ppermute | solution.py:29
  132.6 4.0 %collective-permute-start.12 = (f32[2,6,1,128]{3,2,1,0:T(1,128)S(1)}, f32[2,6,1,128]{3,2,1,0:T(1,128)S(1)}, u32[]{:S(2)}, u32[]{:S(2)}) collective-permute-start(f32[2,6,1,128]{3,2,1,0:T(1,128)S(1)} %get-tuple-element.44), channel_id=1, source_target_pairs={{0,32},{32,64},{64,96},{96,0},{1,33},{33,65},{65,97},{97,1},{2,34}... | collective-permute-start | bytes 18440 | tf_op jit(solution)/shard_map/ppermute | solution.py:26
  136.7 10.4 %collective-permute-start.15 = (f32[2,6,10,1]{3,2,1,0:T(8,128)S(1)}, f32[2,6,10,1]{3,2,1,0:T(8,128)S(1)}, u32[]{:S(2)}, u32[]{:S(2)}) collective-permute-start(f32[2,6,10,1]{3,2,1,0:T(8,128)S(1)} %get-tuple-element.37), channel_id=1, source_target_pairs={{1,0},{2,1},{3,2},{4,3},{5,4},{6,5},{7,6},{8,7},{9,8},{10,9},{11,1... | collective-permute-start | bytes 1448 | tf_op jit(solution)/shard_map/ppermute | solution.py:29
  146.1 1.6 collective-permute-start.14
  148.3 6.5 %collective-permute-start.17 = (f32[2,1,8,128]{3,2,1,0:T(8,128)S(1)}, f32[2,1,8,128]{3,2,1,0:T(8,128)S(1)}, u32[]{:S(2)}, u32[]{:S(2)}) collective-permute-start(f32[2,1,8,128]{3,2,1,0:T(8,128)S(1)} %get-tuple-element.51), channel_id=1, source_target_pairs={{128,0},{0,128},{129,1},{1,129},{130,2},{2,130},{131,3},{3,131},{1... | collective-permute-start | bytes 24584 | tf_op jit(solution)/shard_map/ppermute | solution.py:29
  152.6 6.4 %collective-permute-start.16 = (f32[2,1,8,128]{3,2,1,0:T(8,128)S(1)}, f32[2,1,8,128]{3,2,1,0:T(8,128)S(1)}, u32[]{:S(2)}, u32[]{:S(2)}) collective-permute-start(f32[2,1,8,128]{3,2,1,0:T(8,128)S(1)} %get-tuple-element.50), channel_id=1, source_target_pairs={{0,128},{128,0},{1,129},{129,1},{2,130},{130,2},{3,131},{131,3},{4... | collective-permute-start | bytes 24584 | tf_op jit(solution)/shard_map/ppermute | solution.py:26
  159.0 3.1 %collective-permute-start.19 = (f32[2,6,1,128]{3,2,1,0:T(1,128)S(1)}, f32[2,6,1,128]{3,2,1,0:T(1,128)S(1)}, u32[]{:S(2)}, u32[]{:S(2)}) collective-permute-start(f32[2,6,1,128]{3,2,1,0:T(1,128)S(1)} %get-tuple-element.43), channel_id=1, source_target_pairs={{32,0},{64,32},{96,64},{0,96},{33,1},{65,33},{97,65},{1,97},{34,2}... | collective-permute-start | bytes 18440 | tf_op jit(solution)/shard_map/ppermute | solution.py:29
  159.3 3.8 %collective-permute-start.18 = (f32[2,6,1,128]{3,2,1,0:T(1,128)S(1)}, f32[2,6,1,128]{3,2,1,0:T(1,128)S(1)}, u32[]{:S(2)}, u32[]{:S(2)}) collective-permute-start(f32[2,6,1,128]{3,2,1,0:T(1,128)S(1)} %get-tuple-element.42), channel_id=1, source_target_pairs={{0,32},{32,64},{64,96},{96,0},{1,33},{33,65},{65,97},{97,1},{2,34}... | collective-permute-start | bytes 18440 | tf_op jit(solution)/shard_map/ppermute | solution.py:26
  163.2 11.1 %collective-permute-start.21 = (f32[2,6,10,1]{3,2,1,0:T(8,128)S(1)}, f32[2,6,10,1]{3,2,1,0:T(8,128)S(1)}, u32[]{:S(2)}, u32[]{:S(2)}) collective-permute-start(f32[2,6,10,1]{3,2,1,0:T(8,128)S(1)} %get-tuple-element.35), channel_id=1, source_target_pairs={{1,0},{2,1},{3,2},{4,3},{5,4},{6,5},{7,6},{8,7},{9,8},{10,9},{11,1... | collective-permute-start | bytes 1448 | tf_op jit(solution)/shard_map/ppermute | solution.py:29
  173.4 2.4 %collective-permute-start.20 = (f32[2,6,10,1]{3,2,1,0:T(8,128)S(1)}, f32[2,6,10,1]{3,2,1,0:T(8,128)S(1)}, u32[]{:S(2)}, u32[]{:S(2)}) collective-permute-start(f32[2,6,10,1]{3,2,1,0:T(8,128)S(1)} %get-tuple-element.34), channel_id=1, source_target_pairs={{0,1},{1,2},{2,3},{3,4},{4,5},{5,6},{6,7},{7,8},{8,9},{9,10},{10,1... | collective-permute-start | bytes 1448 | tf_op jit(solution)/shard_map/ppermute | solution.py:26
  176.3 6.5 %collective-permute-start.23 = (f32[2,1,8,128]{3,2,1,0:T(8,128)S(1)}, f32[2,1,8,128]{3,2,1,0:T(8,128)S(1)}, u32[]{:S(2)}, u32[]{:S(2)}) collective-permute-start(f32[2,1,8,128]{3,2,1,0:T(8,128)S(1)} %get-tuple-element.49), channel_id=1, source_target_pairs={{128,0},{0,128},{129,1},{1,129},{130,2},{2,130},{131,3},{3,131},{1... | collective-permute-start | bytes 24584 | tf_op jit(solution)/shard_map/ppermute | solution.py:29
  177.4 6.4 %collective-permute-start.22 = (f32[2,1,8,128]{3,2,1,0:T(8,128)S(1)}, f32[2,1,8,128]{3,2,1,0:T(8,128)S(1)}, u32[]{:S(2)}, u32[]{:S(2)}) collective-permute-start(f32[2,1,8,128]{3,2,1,0:T(8,128)S(1)} %get-tuple-element.48), channel_id=1, source_target_pairs={{0,128},{128,0},{1,129},{129,1},{2,130},{130,2},{3,131},{131,3},{4... | collective-permute-start | bytes 24584 | tf_op jit(solution)/shard_map/ppermute | solution.py:26
  183.9 2.6 %collective-permute-start.25 = (f32[2,6,1,128]{3,2,1,0:T(1,128)S(1)}, f32[2,6,1,128]{3,2,1,0:T(1,128)S(1)}, u32[]{:S(2)}, u32[]{:S(2)}) collective-permute-start(f32[2,6,1,128]{3,2,1,0:T(1,128)S(1)} %get-tuple-element.41), channel_id=1, source_target_pairs={{32,0},{64,32},{96,64},{0,96},{33,1},{65,33},{97,65},{1,97},{34,2}... | collective-permute-start | bytes 18440 | tf_op jit(solution)/shard_map/ppermute | solution.py:29
  183.9 4.1 %collective-permute-start.24 = (f32[2,6,1,128]{3,2,1,0:T(1,128)S(1)}, f32[2,6,1,128]{3,2,1,0:T(1,128)S(1)}, u32[]{:S(2)}, u32[]{:S(2)}) collective-permute-start(f32[2,6,1,128]{3,2,1,0:T(1,128)S(1)} %get-tuple-element.40), channel_id=1, source_target_pairs={{0,32},{32,64},{64,96},{96,0},{1,33},{33,65},{65,97},{97,1},{2,34}... | collective-permute-start | bytes 18440 | tf_op jit(solution)/shard_map/ppermute | solution.py:26
  188.1 9.0 %collective-permute-start.27 = (f32[2,6,10,1]{3,2,1,0:T(8,128)S(1)}, f32[2,6,10,1]{3,2,1,0:T(8,128)S(1)}, u32[]{:S(2)}, u32[]{:S(2)}) collective-permute-start(f32[2,6,10,1]{3,2,1,0:T(8,128)S(1)} %get-tuple-element.33), channel_id=1, source_target_pairs={{1,0},{2,1},{3,2},{4,3},{5,4},{6,5},{7,6},{8,7},{9,8},{10,9},{11,1... | collective-permute-start | bytes 1448 | tf_op jit(solution)/shard_map/ppermute | solution.py:29
  196.2 2.4 %collective-permute-start.26 = (f32[2,6,10,1]{3,2,1,0:T(8,128)S(1)}, f32[2,6,10,1]{3,2,1,0:T(8,128)S(1)}, u32[]{:S(2)}, u32[]{:S(2)}) collective-permute-start(f32[2,6,10,1]{3,2,1,0:T(8,128)S(1)} %get-tuple-element.32), channel_id=1, source_target_pairs={{0,1},{1,2},{2,3},{3,4},{4,5},{5,6},{6,7},{7,8},{8,9},{9,10},{10,1... | collective-permute-start | bytes 1448 | tf_op jit(solution)/shard_map/ppermute | solution.py:26
  (21 other events, 232.8 us)
where the time goes:
time: 204 us; the launch traced here: 200 us
  starting transfers between devices  69.6 us (34%)
  local copies, waits for them, and re-layouts  54.3 us (27%)
  other arithmetic  27.3 us (13%)
  waiting for transfers between devices  24.7 us (12%)
  blocking collectives  21 us (10%)
    ppermute x14, starting transfers between devices, padded_2(): lax.ppermute(lax.slice_in_dim(block, 0, width, axis=dim), axis, backward)  55.9 us
    unnamed x56, local copies, waits for them, and re-layouts  23.5 us
    ppermute x14, waiting for transfers between devices, padded_2(): lax.ppermute(lax.slice_in_dim(block, block.shape[dim] - width, None, axis...  15.7 us
    ppermute x14, starting transfers between devices, padded_2(): lax.ppermute(lax.slice_in_dim(block, block.shape[dim] - width, None, axis...  13.7 us
    psum x1, blocking collectives, shards(): coupling = lax.psum(partial_value, 'sec').reshape(4, tile_rows, tile_cols)  13.3 us
    concatenate x1, local copies, waits for them, and re-layouts, padded_2(): block = jnp.concatenate([low, block, high], axis=dim)  11.9 us
    ppermute x14, waiting for transfers between devices, padded_2(): lax.ppermute(lax.slice_in_dim(block, 0, width, axis=dim), axis, backward)  9.03 us
    psum x1, blocking collectives, broadcast(): return lax.psum(jnp.where(mine, array, jnp.zeros_like(array)), axis)  7.71 us
  transfers between devices with their start and end apart: 28, of which 18 were waited for; matrix products, arithmetic and copies ran while one was open for 24% of the time, Pallas kernels for 0%

commit v1 on v0

v1 whole, which is shorter than its diff:
```python
import functools
import math

import jax
import jax.numpy as jnp
import numpy as np
from jax import lax
from jax.experimental import pallas as pl
from jax.experimental.pallas import tpu as pltpu
from jax.sharding import PartitionSpec as P

ITERS = 4
CURRENT_GAIN = 0.1
STRESS_GAIN = 0.5
MESH = pl.DeviceIdType.MESH
f32 = jnp.float32
CHUNKS = 3


def headings(directions):
    heading = ((np.arange(directions).astype(np.float32) + np.float32(0.5))
               * np.float32(2.0 * math.pi / directions)).astype(np.float64)
    return [float(np.float32(c)) for c in np.cos(heading)], [float(np.float32(s)) for s in np.sin(heading)]


def roll(x, shift, axis):
    shift = shift % x.shape[axis]
    return x if shift == 0 else pltpu.roll(x, shift, axis)


def kernel(
    freqs, dirs, levels, lats, lons,
    spec_hbm, cur_hbm, mask_hbm, diff_hbm, courant, stokes, stress,
    out_spec, out_cur,
    spec, outv, curv, maskv, diffv,
    send_rows, recv_rows, send_cols, recv_cols,
    fld, oth, rowpk, rowpk_in, colpk, colpk_in,
    cpl, cplo, rowc, rowc_in, colc, colc_in,
    dop, ext, ext2, aux, frc, outc,
    local_sem, send_sem, recv_sem,
):
    sec, lat, lon = lax.axis_index("sec"), lax.axis_index("lat"), lax.axis_index("lon")
    north_ok, south_ok = lat < lats - 1, lat > 0
    cosines, sines = headings(dirs)
    east_dirs = [d for d in range(dirs) if cosines[d] > 0]
    west_dirs = [d for d in range(dirs) if cosines[d] <= 0]
    north_dirs = [d for d in range(dirs) if sines[d] > 0]
    south_dirs = [d for d in range(dirs) if sines[d] <= 0]
    half = dirs // 2
    per_chunk = freqs // CHUNKS
    per_group = 128 // half
    groups = -(-freqs // per_group)

    def target(dsec, dlat, dlon):
        return (
            lax.rem(sec + dsec, 2),
            lat + dlat,
            lax.rem(lon + dlon + lons, lons),
        )

    def when_to(dlat, fn):
        if dlat == 0:
            fn()
        else:
            pl.when(north_ok if dlat > 0 else south_ok)(fn)

    partners = [
        (ds, dy, dx) for ds in (0, 1) for dy in (-1, 0, 1) for dx in (-1, 0, 1)
        if (ds, dy, dx) != (0, 0, 0)
    ]
    loads = [
        pltpu.make_async_copy(cur_hbm, curv, local_sem.at[0]),
        pltpu.make_async_copy(mask_hbm, maskv, local_sem.at[1]),
        pltpu.make_async_copy(diff_hbm, diffv, local_sem.at[2]),
        pltpu.make_async_copy(spec_hbm, spec, local_sem.at[3]),
    ]
    for copy in loads:
        copy.start()
    barrier = pltpu.get_barrier_semaphore()
    for ds, dy, dx in partners:
        def greet(ds=ds, dy=dy, dx=dx):
            pl.semaphore_signal(barrier, inc=1, device_id=target(ds, dy, dx), device_id_type=MESH)
        when_to(dy, greet)

    lane = lax.broadcasted_iota(jnp.int32, (8, 128), 1)
    sub = lax.broadcasted_iota(jnp.int32, (8, 128), 0)

    for copy in loads[:3]:
        copy.wait()
    sea = maskv[...].astype(f32)
    for q in range(2):
        for k in range(levels):
            fld[q * levels + k] = curv[q, k] * sea
    fld[2 * levels] = sea
    fld[2 * levels + 1] = diffv[...]
    n_fld = 2 * levels + 2

    def pack_rows(tiles, ref):
        for p in range(len(tiles) // 2):
            a, b = tiles[2 * p], tiles[2 * p + 1]
            ref[0, p] = jnp.where(sub >= 4, b, roll(a, 4, 0))
            ref[1, p] = jnp.where(sub < 4, a, roll(b, 4, 0))

    def pack_cols(tiles, ref):
        to_east = jnp.zeros((8, 128), f32)
        to_west = jnp.zeros((8, 128), f32)
        for i, tile in enumerate(tiles):
            here = (lane >= 4 * i) & (lane < 4 * i + 4)
            to_east = jnp.where(here, roll(tile, 4 * i + 4, 1), to_east)
            to_west = jnp.where(here, roll(tile, 4 * i, 1), to_west)
        ref[0] = to_east
        ref[1] = to_west

    tiles = [fld[i] for i in range(n_fld)]
    pack_rows(tiles, rowpk)
    pack_cols(tiles, colpk)

    loads[3].wait()

    def pack_freq(f, chunk, fi):
        base = f * (dirs * 8)
        for side, first, row in ((0, north_dirs[0], 7), (1, south_dirs[0], 0)):
            for start, count in ((0, 8), (8, 8), (half - 8, 8)):
                at = base + (first + start) * 8 + row
                send_rows[side, chunk, fi * half + start:fi * half + start + count, :] = spec[
                    pl.ds(at, count, stride=8), :
                ]

    for f in range(freqs):
        pack_freq(f, f // per_chunk, f % per_chunk)

    def pack_group(g, _):
        def one(m, accs):
            f = jnp.minimum(g * per_group + m, freqs - 1)
            base = f * (dirs * 8)
            out = []
            for side, chosen, extra in ((0, east_dirs, 1), (1, west_dirs, 0)):
                acc = jnp.zeros((8, 128), f32)
                for j, d in enumerate(chosen):
                    tile = spec[pl.ds(pl.multiple_of(base + d * 8, 8), 8), :]
                    acc = jnp.where(lane == j, roll(tile, j + extra, 1), acc)
                acc = pltpu.roll(acc, half * m, 1)
                here = (lane >= half * m) & (lane < half * m + half)
                out.append(jnp.where(here, acc, accs[side]))
            return tuple(out)

        zero = jnp.zeros((8, 128), f32)
        a, b = lax.fori_loop(0, per_group, one, (zero, zero))
        send_cols[0, g] = a
        send_cols[1, g] = b
        return 0

    lax.fori_loop(0, groups, pack_group, 0)

    edge = jnp.where(north_ok, 0, 6) + jnp.where(south_ok, 0, 6)
    pl.semaphore_wait(barrier, 17 - edge)

    messages = []

    def message(src, dst, ds, dy, dx):
        messages.append((src, dst, ds, dy, dx))
        return len(messages) - 1

    def make(i):
        src, dst, ds, dy, dx = messages[i]
        return pltpu.make_async_remote_copy(
            src_ref=src, dst_ref=dst, send_sem=send_sem.at[i], recv_sem=recv_sem.at[i],
            device_id=target(ds, dy, dx), device_id_type=MESH,
        )

    def start(i):
        when_to(messages[i][3], lambda: make(i).start())

    def wait_recv(i):
        when_to(-messages[i][3], lambda: make(i).wait_recv())

    def wait_send(i):
        when_to(messages[i][3], lambda: make(i).wait_send())

    center = message(fld.at[0:2 * levels], oth, 1, 0, 0)
    cols = [message(send_cols.at[s], recv_cols.at[s], 0, 0, 1 - 2 * s) for s in range(2)]
    rows = [
        [message(send_rows.at[s, c], recv_rows.at[s, c], 0, 1 - 2 * s, 0) for s in range(2)]
        for c in range(CHUNKS)
    ]

    def edge_messages(row_src, row_dst, col_src, col_dst):
        out = []
        for ds in (1, 0):
            for dy in (0, -1, 1):
                for s in range(2):
                    out.append(message(col_src.at[s], col_dst.at[ds, 1 + dy, s], ds, dy, 1 - 2 * s))
            for s in range(2):
                out.append(message(row_src.at[s], row_dst.at[ds, s], ds, 1 - 2 * s, 0))
        return out

    field_edges = edge_messages(rowpk, rowpk_in, colpk, colpk_in)
    for i in [center] + cols + rows[0]:
        start(i)
    for c in range(1, CHUNKS):
        for i in rows[c]:
            start(i)
    for i in field_edges:
        start(i)

    @pl.when(jnp.logical_not(south_ok))
    def _():
        recv_rows[0] = jnp.zeros(recv_rows.shape[1:], f32)

    @pl.when(jnp.logical_not(north_ok))
    def _():
        recv_rows[1] = jnp.zeros(recv_rows.shape[1:], f32)

    wait_recv(center)
    first = sec == 0
    su = jnp.where(first, fld[0], oth[0])
    sv = jnp.where(first, fld[levels], oth[levels])
    for d in range(dirs):
        dop[d] = sea * (1.0 + CURRENT_GAIN * (su * cosines[d] + sv * sines[d]))
    for i in cols:
        wait_recv(i)

    def wave(chunk, fi, sums):
        f = chunk * per_chunk + fi
        base = f * (dirs * 8)
        speed = jnp.full((8, 128), courant[f], f32)
        g = f // per_group
        m = f - g * per_group
        back = lax.rem(128 - half * m, 128)
        from_west = pltpu.roll(recv_cols[0, g], back, 1)
        from_east = pltpu.roll(recv_cols[1, g], back, 1)
        x_sum = jnp.zeros((8, 128), f32)
        y_sum = jnp.zeros((8, 128), f32)
        for d in range(dirs):
            at = pl.ds(pl.multiple_of(base + d * 8, 8), 8)
            tile = spec[at, :]
            if cosines[d] > 0:
                j = east_dirs.index(d)
                beside = jnp.where(lane == 0, roll(from_west, -j, 1), roll(tile, 1, 1))
            else:
                j = west_dirs.index(d)
                beside = jnp.where(lane == 127, roll(from_east, 127 - j, 1), roll(tile, -1, 1))
            if sines[d] > 0:
                row = recv_rows[0, chunk, pl.ds(fi * half + north_dirs.index(d), 1), :]
                along = jnp.where(sub == 0, row, roll(tile, 1, 0))
            else:
                row = recv_rows[1, chunk, pl.ds(fi * half + south_dirs.index(d), 1), :]
                along = jnp.where(sub == 7, row, roll(tile, -1, 0))
            step = abs(cosines[d]) * (beside - tile) + abs(sines[d]) * (along - tile)
            new = (tile + speed * step) * dop[d]
            outv[at, :] = new
            x_sum = x_sum + cosines[d] * new
            y_sum = y_sum + sines[d] * new
        a, b = stokes[f], stress[f]
        return (sums[0] + a * x_sum, sums[1] + a * y_sum, sums[2] + b * x_sum, sums[3] + b * y_sum)

    sums = (jnp.zeros((8, 128), f32),) * 4
    for c in range(CHUNKS):
        for i in rows[c]:
            wait_recv(i)
        sums = lax.fori_loop(0, per_chunk, functools.partial(wave, c), sums)
    store = pltpu.make_async_copy(outv, out_spec, local_sem.at[4])
    store.start()

    for i in range(4):
        cpl[i] = sums[i]
    pack_rows(list(sums), rowc)
    pack_cols(list(sums), colc)
    middle = message(cpl, cplo, 1, 0, 0)
    coupling_edges = [middle] + edge_messages(rowc, rowc_in, colc, colc_in)
    for i in coupling_edges:
        start(i)

    inside = jnp.where(sub < 4, north_ok.astype(jnp.int32), south_ok.astype(jnp.int32)) != 0
    zero = jnp.zeros((8, 128), f32)

    def ghost_rows(from_south, from_north, i):
        p = i // 2
        if i % 2 == 0:
            low, high = roll(from_south[p], 4, 0), from_north[p]
        else:
            low, high = from_south[p], roll(from_north[p], 4, 0)
        return jnp.where(inside, jnp.where(sub < 4, high, low), zero)

    def ghost_lanes(from_west, from_east, i):
        return jnp.where(
            lane < 4,
            roll(from_east, -4 * i, 1),
            jnp.where(lane >= 124, roll(from_west, 124 - 4 * i, 1), zero),
        )

    for i in field_edges:
        wait_recv(i)

    def packs(rows_in, cols_in, r, count):
        from_south = [rows_in[r, 0, p] for p in range(count // 2)]
        from_north = [rows_in[r, 1, p] for p in range(count // 2)]
        side = [cols_in[r, 1, s] for s in range(2)]
        corner = [
            jnp.where(inside, jnp.where(sub < 4, cols_in[r, 0, s], cols_in[r, 2, s]), zero)
            for s in range(2)
        ]
        return from_south, from_north, side, corner

    def place(ref, index, own, got, i):
        from_south, from_north, side, corner = got
        ref[index + (slice(0, 8), slice(0, 128))] = own
        ref[index + (slice(0, 8), slice(128, 256))] = ghost_lanes(side[0], side[1], i)
        ref[index + (slice(8, 16), slice(0, 128))] = ghost_rows(from_south, from_north, i)
        ref[index + (slice(8, 16), slice(128, 256))] = ghost_lanes(corner[0], corner[1], i)

    for r in range(2):
        got = packs(rowpk_in, colpk_in, r, n_fld)
        base = lax.rem(sec + r, 2) * levels
        for q in range(2):
            for k in range(levels):
                i = q * levels + k
                own = fld[i] if r == 0 else oth[i]
                place(ext, (q, base + k), own, got, i)
        if r == 0:
            place(aux, (0,), fld[2 * levels], got, 2 * levels)
            place(aux, (1,), fld[2 * levels + 1], got, 2 * levels + 1)

    total = 2 * levels
    big_sub = lax.broadcasted_iota(jnp.int32, (16, 256), 0)
    row_index = jnp.where(big_sub < 12, big_sub, big_sub - 16) + lat * 8
    aux[2] = 0.05 + 0.1 * (row_index.astype(f32) + 0.5) / (8 * lats)

    def ocean(src, dst, forced):
        def at_level(k, _):
            level = k.astype(f32)
            mix = 0.04 + 0.0125 * lax.rem(7 * k, 5).astype(f32)
            up, down = jnp.maximum(k - 1, 0), jnp.minimum(k + 1, total - 1)
            sea_x, kappa, rot = aux[0], aux[1], aux[2]
            new = []
            center = [src[0, k], src[1, k]]
            for q in range(2):
                mid = center[q]
                lap = (
                    roll(mid, -1, 0) + roll(mid, 1, 0) + roll(mid, -1, 1) + roll(mid, 1, 1)
                    - 4.0 * mid
                )
                vert = mix * ((src[q, up] - mid) + (src[q, down] - mid))
                new.append(mid + kappa * lap + vert)
            new[0] = new[0] + rot * center[1]
            new[1] = new[1] - rot * center[0]
            if forced:
                decay = jnp.full((16, 256), 1.0, f32) / (1.0 + level)
                top = jnp.where(k == 0, STRESS_GAIN, 0.0)
                new[0] = new[0] + decay * frc[1] + top * frc[2]
                new[1] = new[1] - decay * frc[0] + top * frc[3]
            dst[0, k] = sea_x * new[0]
            dst[1, k] = sea_x * new[1]
            return 0

        lax.fori_loop(0, total, at_level, 0)

    ocean(ext, ext2, False)

    for i in coupling_edges:
        wait_recv(i)
    got = [packs(rowc_in, colc_in, r, 4) for r in range(2)]
    both = jax.tree.map(lambda a, b: a + b, got[0], got[1])
    for i in range(4):
        place(frc, (i,), cpl[i] + cplo[i], both, i)
    frc[0] = frc[0] * aux[2]
    frc[1] = frc[1] * aux[2]

    def add_forcing(k, _):
        decay = jnp.full((16, 256), 1.0, f32) / (1.0 + k.astype(f32))
        top = jnp.where(k == 0, STRESS_GAIN, 0.0)
        ext2[0, k] = ext2[0, k] + aux[0] * (decay * frc[1] + top * frc[2])
        ext2[1, k] = ext2[1, k] + aux[0] * (top * frc[3] - decay * frc[0])
        return 0

    lax.fori_loop(0, total, add_forcing, 0)
    src, dst = ext2, ext
    for _ in range(ITERS - 1):
        ocean(src, dst, True)
        src, dst = dst, src
    for q in range(2):
        for k in range(levels):
            outc[q, k] = src[q, sec * levels + k, 0:8, 0:128]
    store_cur = pltpu.make_async_copy(outc, out_cur, local_sem.at[0])
    store_cur.start()
    for i in range(len(messages)):
        wait_send(i)
    store_cur.wait()
    store.wait()


def shards(lats, lons, spectra, currents, land_mask, diffusion, courant, stokes_weight, stress_weight):
    freqs, dirs, tile_rows, tile_cols = spectra.shape
    levels = currents.shape[1]
    cells = freqs * dirs * tile_rows
    half = dirs // 2
    rows = -(-freqs // CHUNKS * half // 8) * 8
    groups = -(-freqs // (128 // half))
    n_fld = 2 * levels + 2
    tile = (8, 128)
    vmem = lambda *shape: pltpu.VMEM(shape, f32)
    any_spec = pl.BlockSpec(memory_space=pl.ANY)
    smem_spec = pl.BlockSpec(memory_space=pltpu.SMEM)
    n_msg = 3 + 2 * CHUNKS + 16 + 17
    new_spectra, new_currents = pl.pallas_call(
        functools.partial(kernel, freqs, dirs, levels, lats, lons),
        out_shape=(
            jax.ShapeDtypeStruct((cells, tile_cols), f32),
            jax.ShapeDtypeStruct(currents.shape, f32),
        ),
        in_specs=[any_spec] * 4 + [smem_spec] * 3,
        out_specs=(any_spec, any_spec),
        scratch_shapes=[
            vmem(cells, 128), vmem(cells, 128), vmem(2, levels, *tile),
            pltpu.VMEM(tile, jnp.int32), vmem(*tile),
            vmem(2, CHUNKS, rows, 128), vmem(2, CHUNKS, rows, 128),
            vmem(2, groups, *tile), vmem(2, groups, *tile),
            vmem(n_fld, *tile), vmem(2 * levels, *tile),
            vmem(2, n_fld // 2, *tile), vmem(2, 2, n_fld // 2, *tile),
            vmem(2, *tile), vmem(2, 3, 2, *tile),
            vmem(4, *tile), vmem(4, *tile),
            vmem(2, 2, *tile), vmem(2, 2, 2, *tile),
            vmem(2, *tile), vmem(2, 3, 2, *tile),
            vmem(dirs, *tile),
            vmem(2, 2 * levels, 16, 256), vmem(2, 2 * levels, 16, 256),
            vmem(3, 16, 256), vmem(4, 16, 256), vmem(2, levels, *tile),
            pltpu.SemaphoreType.DMA((5,)),
            pltpu.SemaphoreType.DMA((n_msg,)),
            pltpu.SemaphoreType.DMA((n_msg,)),
        ],
        compiler_params=pltpu.CompilerParams(collective_id=0, has_side_effects=True),
        name="window",
    )(spectra.reshape(cells, tile_cols), currents, land_mask, diffusion, courant, stokes_weight, stress_weight)
    return new_spectra.reshape(spectra.shape), new_currents


def solution(mesh):
    in_specs = (
        P("sec", None, "lat", "lon"),
        P(None, "sec", "lat", "lon"),
        P("lat", "lon"),
        P("lat", "lon"),
        P("sec"),
        P("sec"),
        P("sec"),
    )
    out_specs = (P("sec", None, "lat", "lon"), P(None, "sec", "lat", "lon"))
    body = functools.partial(shards, mesh.shape["lat"], mesh.shape["lon"])
    return jax.shard_map(body, mesh=mesh, in_specs=in_specs, out_specs=out_specs, check_vma=False)
```

time: 204 us -> 37 us (0.18); the launches traced: 200 us -> 36.8 us
  starting transfers between devices: 69.6 us -> 0 us
  local copies, waits for them, and re-layouts: 54.3 us -> 4.05 us
  Pallas kernels: 0 us -> 32.1 us
  other arithmetic: 27.3 us -> 0 us
  waiting for transfers between devices: 24.7 us -> 0 us
  blocking collectives: 21 us -> 0 us
    ppermute x28 -> x0, starting transfers between devices: 69.6 us -> none  [the longest x14 55.9 us: padded_2(): lax.ppermute(lax.slice_in_dim(block, 0, width, axis=dim), axis, backward)]
    pallas_call x0 -> x1, Pallas kernels: none -> 32.1 us  [shards(): pl.pallas_call(functools.partial(kernel, freqs, dirs, levels, lats, lons)...]
    ppermute x28 -> x0, waiting for transfers between devices: 24.7 us -> none  [the longest x14 15.7 us: padded_2(): lax.ppermute(lax.slice_in_dim(block, block.shape[dim] - width, None, axis...]
    psum x2 -> x0, blocking collectives: 21 us -> none  [the longest x1 13.3 us: shards(): coupling = lax.psum(partial_value, 'sec').reshape(4, tile_rows, tile_cols)]
    unnamed x56 -> x4, local copies, waits for them, and re-layouts: 23.5 us -> 4.05 us
    mul x13 -> x0, other arithmetic: 12.8 us -> none  [the longest x1 7.7 us: wave_update(): return sea_cells * (advected * doppler)]
    concatenate x1 -> x0, local copies, waits for them, and re-layouts: 11.9 us -> none  [padded_2(): block = jnp.concatenate([low, block, high], axis=dim)]
    ppermute x4 -> x0, local copies, waits for them, and re-layouts: 10.5 us -> none  [the longest x2 5.26 us: padded_2(): lax.ppermute(lax.slice_in_dim(block, 0, width, axis=dim), axis, backward)]
  transfers between devices with their start and end apart: 28 -> 0, of which waited for: 18 -> 0; matrix products, arithmetic and copies ran while one was open for 24% -> 0% of each run, Pallas kernels for 0% -> 0%
where the time goes in v1:
time: 37 us; the launch traced here: 36.8 us
  Pallas kernels  32.1 us (87%)
  local copies, waits for them, and re-layouts  4.05 us (11%)
  between operations  0.65 us (2%)
    pallas_call x1, Pallas kernels, shards(): pl.pallas_call(functools.partial(kernel, freqs, dirs, levels, lats, lons)...  32.1 us
    unnamed x4, local copies, waits for them, and re-layouts  4.05 us

profile of v1, /device:TPU:1, one launch (start us, length us, event | category | flops | bytes accessed | tf_op | source)
XLA Modules:
  0.0 36.8 jit_solution(2949950308180101314)
XLA Ops:
  0.6 32.1 %window.1 = (f32[5184,128]{1,0:T(8,128)}, f32[2,4,8,128]{3,2,1,0:T(8,128)}) custom-call(f32[5184,128]{1,0:T(8,128)} %bitcast.2, f32[2,4,8,128]{3,2,1,0:T(8,128)} %cur_hbm.1, s32[8,128]{1,0:T(8,128)} %mask_hbm.1, f32[8,128]{1,0:T(8,128)} %diff_hbm.1, f32[18]{0:T(128)} %courant.1, f32[18]{0:T(128)} %stokes.1, f32[18]{0:T(128)} %stress.1), custom_call_target="tpu_custom_call" | custom-call | tf_op jit(solution)/shard_map/window/pallas_call | solution.py:405
  32.8 0.0 copy-start
  32.8 3.4 %copy.11 = f32[18,36,8,128]{3,2,1,0:T(8,128)} copy(f32[18,36,8,128]{3,2,1,0:T(8,128)} %bitcast.3) | data formatting | bytes 5308416
  36.2 0.0 copy-done
  36.2 0.6 %copy.12 = f32[2,4,8,128]{3,2,1,0:T(8,128)} copy(f32[2,4,8,128]{3,2,1,0:T(8,128)S(1)} %copy-done) | data formatting | bytes 65536
Async XLA Ops:
  32.8 3.4 %copy-start = (f32[2,4,8,128]{3,2,1,0:T(8,128)S(1)}, f32[2,4,8,128]{3,2,1,0:T(8,128)}, u32[]{:S(2)}) copy-start(f32[2,4,8,128]{3,2,1,0:T(8,128)} %get-tuple-element.9) | copy-start | bytes 98308

commit v2 on v1

--- a/solution.py
+++ b/solution.py
@@ -15,6 +15,7 @@
 MESH = pl.DeviceIdType.MESH
 f32 = jnp.float32
 CHUNKS = 3
+EMIT = 4
 
 
 def headings(directions):
@@ -30,13 +31,13 @@
 
 def kernel(
     freqs, dirs, levels, lats, lons,
-    spec_hbm, cur_hbm, mask_hbm, diff_hbm, courant, stokes, stress,
-    out_spec, out_cur,
-    spec, outv, curv, maskv, diffv,
+    spec_hbm, cur_hbm, mask_hbm, diff_hbm, courant_hbm, stokes_hbm, stress_hbm,
+    out_spec, ext2, aux, frc,
+    spec, curv, maskv, diffv, courant, stokes, stress, table,
     send_rows, recv_rows, send_cols, recv_cols,
     fld, oth, rowpk, rowpk_in, colpk, colpk_in,
     cpl, cplo, rowc, rowc_in, colc, colc_in,
-    dop, ext, ext2, aux, frc, outc,
+    dop, acc, ext, pats, rims,
     local_sem, send_sem, recv_sem,
 ):
     sec, lat, lon = lax.axis_index("sec"), lax.axis_index("lat"), lax.axis_index("lon")
@@ -73,6 +74,9 @@
         pltpu.make_async_copy(mask_hbm, maskv, local_sem.at[1]),
         pltpu.make_async_copy(diff_hbm, diffv, local_sem.at[2]),
         pltpu.make_async_copy(spec_hbm, spec, local_sem.at[3]),
+        pltpu.make_async_copy(courant_hbm, courant, local_sem.at[4]),
+        pltpu.make_async_copy(stokes_hbm, stokes, local_sem.at[5]),
+        pltpu.make_async_copy(stress_hbm, stress, local_sem.at[6]),
     ]
     for copy in loads:
         copy.start()
@@ -152,6 +156,27 @@
 
     lax.fori_loop(0, groups, pack_group, 0)
 
+    for copy in loads[4:]:
+        copy.wait()
+    member = lane // half
+    place_in = lane - member * half
+    for g in range(groups):
+        for n, ref in enumerate((courant, stokes, stress)):
+            value = jnp.zeros((8, 128), f32)
+            for m in range(per_group):
+                if g * per_group + m < freqs:
+                    value = jnp.where(member == m, ref[g * per_group + m], value)
+            pats[n * groups + g] = value
+    for side, chosen in enumerate((east_dirs, west_dirs)):
+        for n, values in enumerate((cosines, sines)):
+            value = jnp.zeros((8, 128), f32)
+            for j, d in enumerate(chosen):
+                value = jnp.where(place_in == j, values[d], value)
+            pats[3 * groups + 2 * side + n] = value
+    for d in range(dirs):
+        table[0, d] = abs(cosines[d])
+        table[1, d] = abs(sines[d])
+
     edge = jnp.where(north_ok, 0, 6) + jnp.where(south_ok, 0, 6)
     pl.semaphore_wait(barrier, 17 - edge)
 
@@ -211,65 +236,116 @@
     def _():
         recv_rows[1] = jnp.zeros(recv_rows.shape[1:], f32)
 
+    quadrants = []
+    for d in range(dirs):
+        kind = (cosines[d] > 0, sines[d] > 0)
+        if quadrants and quadrants[-1][0] == kind:
+            quadrants[-1][2] += 1
+        else:
+            quadrants.append([kind, d, 1])
+
+    def wave(chunk):
+        f0 = chunk * per_chunk
+        speeds = [jnp.full((8, 128), courant[f0 + i], f32) for i in range(per_chunk)]
+        firsts = [jnp.full((8, 128), stokes[f0 + i], f32) for i in range(per_chunk)]
+        seconds = [jnp.full((8, 128), stress[f0 + i], f32) for i in range(per_chunk)]
+        for (to_east, to_north), d0, count in quadrants:
+            group = max(g for g in range(1, 4) if count % g == 0)
+            rim = 0 if to_north else 1
+            row0 = (north_dirs if to_north else south_dirs)[0]
+
+            def body(step, _):
+                for n in range(group):
+                    d = d0 + step * group + n
+                    along_x, along_y = table[0, d], table[1, d]
+                    if chunk == 0:
+                        a1 = jnp.zeros((8, 128), f32)
+                        a2 = jnp.zeros((8, 128), f32)
+                    else:
+                        a1, a2 = acc[0, d], acc[1, d]
+                    for fi in range(per_chunk):
+                        at = pl.ds(pl.multiple_of((f0 + fi) * dirs * 8 + d * 8, 8), 8)
+                        tile = spec[at, :]
+                        beside = roll(tile, 1 if to_east else -1, 1)
+                        row = recv_rows[rim, chunk, pl.ds(fi * half + d - row0, 1), :]
+                        if to_north:
+                            along = jnp.where(sub == 0, row, roll(tile, 1, 0))
+                        else:
+                            along = jnp.where(sub == 7, row, roll(tile, -1, 0))
+                        change = along_x * (beside - tile) + along_y * (along - tile)
+                        moved = tile + speeds[fi] * change
+                        out_spec[at, :] = moved
+                        a1 = a1 + firsts[fi] * moved
+                        a2 = a2 + seconds[fi] * moved
+                    acc[0, d] = a1
+                    acc[1, d] = a2
+                return 0
+
+            lax.fori_loop(0, count // group, body, 0)
+
+    for c in range(CHUNKS):
+        for i in rows[c]:
+            wait_recv(i)
+        wave(c)
+
     wait_recv(center)
     first = sec == 0
     su = jnp.where(first, fld[0], oth[0])
     sv = jnp.where(first, fld[levels], oth[levels])
+    sums = [jnp.zeros((8, 128), f32)] * 4
     for d in range(dirs):
-        dop[d] = sea * (1.0 + CURRENT_GAIN * (su * cosines[d] + sv * sines[d]))
+        factor = sea * (1.0 + CURRENT_GAIN * (su * cosines[d] + sv * sines[d]))
+        dop[d] = factor
+        a1, a2 = factor * acc[0, d], factor * acc[1, d]
+        sums[0] = sums[0] + cosines[d] * a1
+        sums[1] = sums[1] + sines[d] * a1
+        sums[2] = sums[2] + cosines[d] * a2
+        sums[3] = sums[3] + sines[d] * a2
+
     for i in cols:
         wait_recv(i)
-
-    def wave(chunk, fi, sums):
-        f = chunk * per_chunk + fi
-        base = f * (dirs * 8)
-        speed = jnp.full((8, 128), courant[f], f32)
-        g = f // per_group
-        m = f - g * per_group
-        back = lax.rem(128 - half * m, 128)
-        from_west = pltpu.roll(recv_cols[0, g], back, 1)
-        from_east = pltpu.roll(recv_cols[1, g], back, 1)
-        x_sum = jnp.zeros((8, 128), f32)
-        y_sum = jnp.zeros((8, 128), f32)
-        for d in range(dirs):
-            at = pl.ds(pl.multiple_of(base + d * 8, 8), 8)
-            tile = spec[at, :]
-            if cosines[d] > 0:
-                j = east_dirs.index(d)
-                beside = jnp.where(lane == 0, roll(from_west, -j, 1), roll(tile, 1, 1))
-            else:
-                j = west_dirs.index(d)
-                beside = jnp.where(lane == 127, roll(from_east, 127 - j, 1), roll(tile, -1, 1))
-            if sines[d] > 0:
-                row = recv_rows[0, chunk, pl.ds(fi * half + north_dirs.index(d), 1), :]
-                along = jnp.where(sub == 0, row, roll(tile, 1, 0))
-            else:
-                row = recv_rows[1, chunk, pl.ds(fi * half + south_dirs.index(d), 1), :]
-                along = jnp.where(sub == 7, row, roll(tile, -1, 0))
-            step = abs(cosines[d]) * (beside - tile) + abs(sines[d]) * (along - tile)
-            new = (tile + speed * step) * dop[d]
-            outv[at, :] = new
-            x_sum = x_sum + cosines[d] * new
-            y_sum = y_sum + sines[d] * new
-        a, b = stokes[f], stress[f]
-        return (sums[0] + a * x_sum, sums[1] + a * y_sum, sums[2] + b * x_sum, sums[3] + b * y_sum)
-
-    sums = (jnp.zeros((8, 128), f32),) * 4
-    for c in range(CHUNKS):
-        for i in rows[c]:
-            wait_recv(i)
-        sums = lax.fori_loop(0, per_chunk, functools.partial(wave, c), sums)
-    store = pltpu.make_async_copy(outv, out_spec, local_sem.at[4])
-    store.start()
+    for side in range(2):
+        at = 0 if side == 0 else 127
+        cos_l, sin_l = pats[3 * groups + 2 * side], pats[3 * groups + 2 * side + 1]
+        wide = lambda x: jnp.broadcast_to(x[:, at:at + 1], (8, 128))
+        factor = wide(sea) * (1.0 + CURRENT_GAIN * (wide(su) * cos_l + wide(sv) * sin_l))
+        s1 = jnp.zeros((8, 128), f32)
+        s2 = jnp.zeros((8, 128), f32)
+        for g in range(groups):
+            rim = pats[g] * jnp.abs(cos_l) * (recv_cols[side, g] - send_cols[side, g])
+            rims[side, g] = rim
+            s1 = s1 + pats[groups + g] * (rim * factor)
+            s2 = s2 + pats[2 * groups + g] * (rim * factor)
+        for n, part in enumerate((s1 * cos_l, s1 * sin_l, s2 * cos_l, s2 * sin_l)):
+            extra = jnp.broadcast_to(jnp.sum(part, axis=1, keepdims=True), (8, 128))
+            sums[n] = sums[n] + jnp.where(lane == at, extra, 0.0)
 
     for i in range(4):
         cpl[i] = sums[i]
-    pack_rows(list(sums), rowc)
-    pack_cols(list(sums), colc)
+    pack_rows(sums, rowc)
+    pack_cols(sums, colc)
     middle = message(cpl, cplo, 1, 0, 0)
     coupling_edges = [middle] + edge_messages(rowc, rowc_in, colc, colc_in)
     for i in coupling_edges:
         start(i)
+
+    def finish(f, _):
+        base = f * (dirs * 8)
+        g = f // per_group
+        m = f - g * per_group
+        back = lax.rem(128 - half * m, 128)
+        from_west = pltpu.roll(rims[0, g], back, 1)
+        from_east = pltpu.roll(rims[1, g], back, 1)
+        for d in range(dirs):
+            at = pl.ds(pl.multiple_of(base + d * 8, 8), 8)
+            if cosines[d] > 0:
+                extra = jnp.where(lane == 0, roll(from_west, -east_dirs.index(d), 1), 0.0)
+            else:
+                extra = jnp.where(lane == 127, roll(from_east, 127 - west_dirs.index(d), 1), 0.0)
+            out_spec[at, :] = (out_spec[at, :] + extra) * dop[d]
+        return 0
+
+    lax.fori_loop(0, freqs, finish, 0)
 
     inside = jnp.where(sub < 4, north_ok.astype(jnp.int32), south_ok.astype(jnp.int32)) != 0
     zero = jnp.zeros((8, 128), f32)
@@ -311,51 +387,28 @@
 
     for r in range(2):
         got = packs(rowpk_in, colpk_in, r, n_fld)
-        base = lax.rem(sec + r, 2) * levels
         for q in range(2):
             for k in range(levels):
                 i = q * levels + k
                 own = fld[i] if r == 0 else oth[i]
-                place(ext, (q, base + k), own, got, i)
+                position = r * levels + jnp.where(first, k, levels - 1 - k)
+                place(ext, (q, position), own, got, i)
         if r == 0:
             place(aux, (0,), fld[2 * levels], got, 2 * levels)
             place(aux, (1,), fld[2 * levels + 1], got, 2 * levels + 1)
 
-    total = 2 * levels
     big_sub = lax.broadcasted_iota(jnp.int32, (16, 256), 0)
     row_index = jnp.where(big_sub < 12, big_sub, big_sub - 16) + lat * 8
     aux[2] = 0.05 + 0.1 * (row_index.astype(f32) + 0.5) / (8 * lats)
 
-    def ocean(src, dst, forced):
-        def at_level(k, _):
-            level = k.astype(f32)
-            mix = 0.04 + 0.0125 * lax.rem(7 * k, 5).astype(f32)
-            up, down = jnp.maximum(k - 1, 0), jnp.minimum(k + 1, total - 1)
-            sea_x, kappa, rot = aux[0], aux[1], aux[2]
-            new = []
-            center = [src[0, k], src[1, k]]
-            for q in range(2):
-                mid = center[q]
-                lap = (
-                    roll(mid, -1, 0) + roll(mid, 1, 0) + roll(mid, -1, 1) + roll(mid, 1, 1)
-                    - 4.0 * mid
-                )
-                vert = mix * ((src[q, up] - mid) + (src[q, down] - mid))
-                new.append(mid + kappa * lap + vert)
-            new[0] = new[0] + rot * center[1]
-            new[1] = new[1] - rot * center[0]
-            if forced:
-                decay = jnp.full((16, 256), 1.0, f32) / (1.0 + level)
-                top = jnp.where(k == 0, STRESS_GAIN, 0.0)
-                new[0] = new[0] + decay * frc[1] + top * frc[2]
-                new[1] = new[1] - decay * frc[0] + top * frc[3]
-            dst[0, k] = sea_x * new[0]
-            dst[1, k] = sea_x * new[1]
-            return 0
-
-        lax.fori_loop(0, total, at_level, 0)
-
-    ocean(ext, ext2, False)
+    total = 2 * levels
+
+    def at_level(p, _):
+        ocean_level(ext, ext2, aux, None, first, total, p)
+        return 0
+
+    ocean_level(ext, ext2, aux, None, first, total, 0)
+    lax.fori_loop(1, total - 1, at_level, 0)
 
     for i in coupling_edges:
         wait_recv(i)
@@ -363,30 +416,72 @@
     both = jax.tree.map(lambda a, b: a + b, got[0], got[1])
     for i in range(4):
         place(frc, (i,), cpl[i] + cplo[i], both, i)
-    frc[0] = frc[0] * aux[2]
-    frc[1] = frc[1] * aux[2]
-
-    def add_forcing(k, _):
-        decay = jnp.full((16, 256), 1.0, f32) / (1.0 + k.astype(f32))
-        top = jnp.where(k == 0, STRESS_GAIN, 0.0)
-        ext2[0, k] = ext2[0, k] + aux[0] * (decay * frc[1] + top * frc[2])
-        ext2[1, k] = ext2[1, k] + aux[0] * (top * frc[3] - decay * frc[0])
-        return 0
-
-    lax.fori_loop(0, total, add_forcing, 0)
-    src, dst = ext2, ext
-    for _ in range(ITERS - 1):
-        ocean(src, dst, True)
-        src, dst = dst, src
-    for q in range(2):
-        for k in range(levels):
-            outc[q, k] = src[q, sec * levels + k, 0:8, 0:128]
-    store_cur = pltpu.make_async_copy(outc, out_cur, local_sem.at[0])
-    store_cur.start()
     for i in range(len(messages)):
         wait_send(i)
-    store_cur.wait()
-    store.wait()
+
+
+def level_of(first, total, p):
+    return jnp.where(first, p, total - 1 - p)
+
+
+def forcing(aux, frc, first, total, p):
+    k = level_of(first, total, p)
+    decay = aux[2] / (1.0 + k.astype(f32))
+    top = jnp.where(k == 0, STRESS_GAIN, 0.0)
+    return decay * frc[1] + top * frc[2], top * frc[3] - decay * frc[0]
+
+
+def ocean_level(src, dst, aux, frc, first, total, p):
+    k = level_of(first, total, p)
+    mix = 0.04 + 0.0125 * lax.rem(7 * k, 5).astype(f32)
+    center = [src[0, p], src[1, p]]
+    new = []
+    for q in range(2):
+        mid = center[q]
+        lap = (
+            roll(mid, -1, 0) + roll(mid, 1, 0) + roll(mid, -1, 1) + roll(mid, 1, 1) - 4.0 * mid
+        )
+        vert = src[q, p + 1] - mid
+        if not (isinstance(p, int) and p == 0):
+            vert = vert + (src[q, p - 1] - mid)
+        new.append(mid + aux[1] * lap + mix * vert)
+    new[0] = new[0] + aux[2] * center[1]
+    new[1] = new[1] - aux[2] * center[0]
+    if frc is not None:
+        force = forcing(aux, frc, first, total, p)
+        new = [new[0] + force[0], new[1] + force[1]]
+    for q in range(2):
+        if dst.shape[-1] == 256:
+            dst[q, p] = aux[0] * new[q]
+        else:
+            own = jnp.where(first, p, dst.shape[1] - 1 - p)
+            dst[q, own] = (aux[0] * new[q])[0:8, 0:128]
+
+
+def emit(levels, spec, ext2, aux, frc, out_spec, out_cur, fa, fb, cur, sems):
+    part = spec.shape[0] // EMIT
+    copies = []
+    for i in range(EMIT):
+        at = pl.ds(i * part, part)
+        copies.append(pltpu.make_async_copy(spec.at[at], out_spec.at[at], sems.at[i]))
+    for copy in copies:
+        copy.start()
+    first = lax.axis_index("sec") == 0
+    total = 2 * levels
+    for p in range(total - 1):
+        force = forcing(aux, frc, first, total, p)
+        for q in range(2):
+            fa[q, p] = ext2[q, p] + aux[0] * force[q]
+    src, dst = fa, fb
+    for step in range(1, ITERS):
+        for p in range(total - 1 - step):
+            ocean_level(src, cur if step == ITERS - 1 else dst, aux, frc, first, total, p)
+        src, dst = dst, src
+    last = pltpu.make_async_copy(cur, out_cur, sems.at[EMIT])
+    last.start()
+    for copy in copies:
+        copy.wait()
+    last.wait()
 
 
 def shards(lats, lons, spectra, currents, land_mask, diffusion, courant, stokes_weight, stress_weight):
@@ -400,19 +495,19 @@
     tile = (8, 128)
     vmem = lambda *shape: pltpu.VMEM(shape, f32)
     any_spec = pl.BlockSpec(memory_space=pl.ANY)
-    smem_spec = pl.BlockSpec(memory_space=pltpu.SMEM)
     n_msg = 3 + 2 * CHUNKS + 16 + 17
-    new_spectra, new_currents = pl.pallas_call(
+    big = (2, 2 * levels, 16, 256)
+    vmem_spec = pl.BlockSpec(memory_space=pltpu.VMEM)
+    results = pl.pallas_call(
         functools.partial(kernel, freqs, dirs, levels, lats, lons),
-        out_shape=(
-            jax.ShapeDtypeStruct((cells, tile_cols), f32),
-            jax.ShapeDtypeStruct(currents.shape, f32),
-        ),
-        in_specs=[any_spec] * 4 + [smem_spec] * 3,
-        out_specs=(any_spec, any_spec),
+        out_shape=(vmem(cells, 128), vmem(*big), vmem(3, 16, 256), vmem(4, 16, 256)),
+        in_specs=[any_spec] * 7,
+        out_specs=(vmem_spec,) * 4,
         scratch_shapes=[
-            vmem(cells, 128), vmem(cells, 128), vmem(2, levels, *tile),
+            vmem(cells, 128), vmem(2, levels, *tile),
             pltpu.VMEM(tile, jnp.int32), vmem(*tile),
+            pltpu.SMEM((freqs,), f32), pltpu.SMEM((freqs,), f32), pltpu.SMEM((freqs,), f32),
+            pltpu.SMEM((2, dirs), f32),
             vmem(2, CHUNKS, rows, 128), vmem(2, CHUNKS, rows, 128),
             vmem(2, groups, *tile), vmem(2, groups, *tile),
             vmem(n_fld, *tile), vmem(2 * levels, *tile),
@@ -421,16 +516,29 @@
             vmem(4, *tile), vmem(4, *tile),
             vmem(2, 2, *tile), vmem(2, 2, 2, *tile),
             vmem(2, *tile), vmem(2, 3, 2, *tile),
-            vmem(dirs, *tile),
-            vmem(2, 2 * levels, 16, 256), vmem(2, 2 * levels, 16, 256),
-            vmem(3, 16, 256), vmem(4, 16, 256), vmem(2, levels, *tile),
-            pltpu.SemaphoreType.DMA((5,)),
+            vmem(dirs, *tile), vmem(2, dirs, *tile), vmem(*big),
+            vmem(3 * groups + 4, *tile), vmem(2, groups, *tile),
+            pltpu.SemaphoreType.DMA((7,)),
             pltpu.SemaphoreType.DMA((n_msg,)),
             pltpu.SemaphoreType.DMA((n_msg,)),
         ],
         compiler_params=pltpu.CompilerParams(collective_id=0, has_side_effects=True),
         name="window",
     )(spectra.reshape(cells, tile_cols), currents, land_mask, diffusion, courant, stokes_weight, stress_weight)
+    results = [pltpu.with_memory_space_constraint(r, pltpu.VMEM) for r in results]
+    new_spectra, new_currents = pl.pallas_call(
+        functools.partial(emit, levels),
+        out_shape=(
+            jax.ShapeDtypeStruct((cells, tile_cols), f32),
+            jax.ShapeDtypeStruct(currents.shape, f32),
+        ),
+        in_specs=[vmem_spec] * 4,
+        out_specs=(any_spec, any_spec),
+        scratch_shapes=[
+            vmem(*big), vmem(*big), vmem(2, levels, *tile), pltpu.SemaphoreType.DMA((EMIT + 1,)),
+        ],
+        name="emit",
+    )(*results)
     return new_spectra.reshape(spectra.shape), new_currents
 
 

time: 37 us -> 28.6 us (0.77)
  Pallas kernels: 32.1 us -> 27.9 us
  local copies, waits for them, and re-layouts: 4.05 us -> 0 us
    pallas_call x1, Pallas kernels: 32.1 us -> 26.3 us  [shards(): pl.pallas_call(functools.partial(kernel, freqs, dirs, levels, lats, lons)...]
    unnamed x4 -> x0, local copies, waits for them, and re-layouts: 4.05 us -> none
    pallas_call x0 -> x1, Pallas kernels: none -> 1.59 us  [shards(): pl.pallas_call(functools.partial(emit, levels), out_shape=(jax.ShapeDtype...]
where the time goes in v2:
time: 28.6 us; the launch traced here: 28.5 us
  Pallas kernels  27.9 us (98%)
  between operations  0.64 us (2%)
    pallas_call x1, Pallas kernels, shards(): pl.pallas_call(functools.partial(kernel, freqs, dirs, levels, lats, lons)...  26.3 us
    pallas_call x1, Pallas kernels, shards(): pl.pallas_call(functools.partial(emit, levels), out_shape=(jax.ShapeDtype...  1.59 us

profile of v2, /device:TPU:1, one launch (start us, length us, event | category | flops | bytes accessed | tf_op | source)
XLA Modules:
  0.0 28.5 jit_solution(11747327862615708004)
XLA Ops:
  0.6 26.3 %window.1 = (f32[5184,128]{1,0:T(8,128)S(1)}, f32[2,8,16,256]{3,2,1,0:T(8,128)S(1)}, f32[3,16,256]{2,1,0:T(8,128)S(1)}, f32[4,16,256]{2,1,0:T(8,128)S(1)}) custom-call(f32[5184,128]{1,0:T(8,128)} %bitcast.2, f32[2,4,8,128]{3,2,1,0:T(8,128)} %cur_hbm.1, s32[8,128]{1,0:T(8,128)} %mask_hbm.1, f32[8,128]{1,0:T(8,128)} %diff_hbm.1, f32[18]{0:T(128)} %courant_hbm.1, ...), custom_call_target="tpu_custom_call" | custom-call | tf_op jit(solution)/shard_map/window/pallas_call | solution.py:501
  26.9 1.6 %emit.1 = (f32[5184,128]{1,0:T(8,128)}, f32[2,4,8,128]{3,2,1,0:T(8,128)}) custom-call(f32[5184,128]{1,0:T(8,128)S(1)} %get-tuple-element.8.spec, f32[2,8,16,256]{3,2,1,0:T(8,128)S(1)} %get-tuple-element.9.ext2, f32[3,16,256]{2,1,0:T(8,128)S(1)} %get-tuple-element.10.aux, f32[4,16,256]{2,1,0:T(8,128)S(1)} %get-tuple-element.11.frc), custom_call_target="tpu_custom_call" | custom-call | tf_op jit(solution)/shard_map/emit/pallas_call | solution.py:529

commit v3 on v2

--- a/solution.py
+++ b/solution.py
@@ -35,10 +35,10 @@
     out_spec, ext2, aux, frc,
     spec, curv, maskv, diffv, courant, stokes, stress, table,
     send_rows, recv_rows, send_cols, recv_cols,
-    fld, oth, rowpk, rowpk_in, colpk, colpk_in,
+    own, oth, edges, rowpk, row_in, colpk, col_in,
     cpl, cplo, rowc, rowc_in, colc, colc_in,
-    dop, acc, ext, pats, rims,
-    local_sem, send_sem, recv_sem,
+    dop, acc, gsum, sums, hrow, hrow_in, hcol, hcol_in, ext,
+    local_sem, send_sem, recv_sem, ready,
 ):
     sec, lat, lon = lax.axis_index("sec"), lax.axis_index("lat"), lax.axis_index("lon")
     north_ok, south_ok = lat < lats - 1, lat > 0
@@ -67,7 +67,7 @@
 
     partners = [
         (ds, dy, dx) for ds in (0, 1) for dy in (-1, 0, 1) for dx in (-1, 0, 1)
-        if (ds, dy, dx) != (0, 0, 0)
+        if (ds, dy, dx) == (1, 0, 0) or (ds == 0 and (dy, dx) != (0, 0))
     ]
     loads = [
         pltpu.make_async_copy(cur_hbm, curv, local_sem.at[0]),
@@ -89,43 +89,24 @@
     lane = lax.broadcasted_iota(jnp.int32, (8, 128), 1)
     sub = lax.broadcasted_iota(jnp.int32, (8, 128), 0)
 
+    first = sec == 0
     for copy in loads[:3]:
         copy.wait()
     sea = maskv[...].astype(f32)
     for q in range(2):
-        for k in range(levels):
-            fld[q * levels + k] = curv[q, k] * sea
-    fld[2 * levels] = sea
-    fld[2 * levels + 1] = diffv[...]
-    n_fld = 2 * levels + 2
-
-    def pack_rows(tiles, ref):
-        for p in range(len(tiles) // 2):
-            a, b = tiles[2 * p], tiles[2 * p + 1]
-            ref[0, p] = jnp.where(sub >= 4, b, roll(a, 4, 0))
-            ref[1, p] = jnp.where(sub < 4, a, roll(b, 4, 0))
-
-    def pack_cols(tiles, ref):
-        to_east = jnp.zeros((8, 128), f32)
-        to_west = jnp.zeros((8, 128), f32)
-        for i, tile in enumerate(tiles):
-            here = (lane >= 4 * i) & (lane < 4 * i + 4)
-            to_east = jnp.where(here, roll(tile, 4 * i + 4, 1), to_east)
-            to_west = jnp.where(here, roll(tile, 4 * i, 1), to_west)
-        ref[0] = to_east
-        ref[1] = to_west
-
-    tiles = [fld[i] for i in range(n_fld)]
-    pack_rows(tiles, rowpk)
-    pack_cols(tiles, colpk)
+        for p in range(levels):
+            own[q * levels + p] = curv[q, jnp.where(first, p, levels - 1 - p)] * sea
+    edges[0] = sea
+    edges[1] = diffv[...]
+    n_fld, n_sum = 2 * levels, 10
 
     loads[3].wait()
 
     def pack_freq(f, chunk, fi):
         base = f * (dirs * 8)
-        for side, first, row in ((0, north_dirs[0], 7), (1, south_dirs[0], 0)):
+        for side, start_dir, row in ((0, north_dirs[0], 7), (1, south_dirs[0], 0)):
             for start, count in ((0, 8), (8, 8), (half - 8, 8)):
-                at = base + (first + start) * 8 + row
+                at = base + (start_dir + start) * 8 + row
                 send_rows[side, chunk, fi * half + start:fi * half + start + count, :] = spec[
                     pl.ds(at, count, stride=8), :
                 ]
@@ -158,27 +139,96 @@
 
     for copy in loads[4:]:
         copy.wait()
-    member = lane // half
-    place_in = lane - member * half
-    for g in range(groups):
-        for n, ref in enumerate((courant, stokes, stress)):
-            value = jnp.zeros((8, 128), f32)
-            for m in range(per_group):
-                if g * per_group + m < freqs:
-                    value = jnp.where(member == m, ref[g * per_group + m], value)
-            pats[n * groups + g] = value
-    for side, chosen in enumerate((east_dirs, west_dirs)):
-        for n, values in enumerate((cosines, sines)):
-            value = jnp.zeros((8, 128), f32)
-            for j, d in enumerate(chosen):
-                value = jnp.where(place_in == j, values[d], value)
-            pats[3 * groups + 2 * side + n] = value
     for d in range(dirs):
         table[0, d] = abs(cosines[d])
         table[1, d] = abs(sines[d])
-
-    edge = jnp.where(north_ok, 0, 6) + jnp.where(south_ok, 0, 6)
-    pl.semaphore_wait(barrier, 17 - edge)
+    group = 3
+
+    def weigh(step, _):
+        total = [[jnp.zeros((8, 128), f32)] * 4 for _ in range(group)]
+        for f in range(freqs):
+            a, b, c = stokes[f], stress[f], courant[f]
+            ws = [jnp.full((8, 128), w, f32) for w in (a, b, a * c, b * c)]
+            for n in range(group):
+                at = f * dirs * 8 + (step * group + n) * 8
+                tile = spec[pl.ds(pl.multiple_of(at, 8), 8), :]
+                total[n] = [t + w * tile for t, w in zip(total[n], ws)]
+        for n in range(group):
+            for i in range(4):
+                acc[i, step * group + n] = total[n][i]
+        return 0
+
+    lax.fori_loop(0, dirs // group, weigh, 0)
+
+    zero = jnp.zeros((8, 128), f32)
+    bases = [
+        (c, s, c * c, c * s, s * s) for c, s in zip(cosines, sines)
+    ]
+    north, south, east, west = [], [], [], []
+    for w in range(2):
+        mid = [zero] * 5
+        ns = [[zero] * 5, [zero] * 5]
+        ew = [[zero] * 5, [zero] * 5]
+        for d in range(dirs):
+            plain, moved = acc[w, d], acc[2 + w, d]
+            along_x, along_y = abs(cosines[d]), abs(sines[d])
+            kept = plain - (along_x + along_y) * moved
+            to_x, to_y = along_x * moved, along_y * moved
+            x, y = 0 if cosines[d] > 0 else 1, 0 if sines[d] > 0 else 1
+            for m in range(5):
+                mid[m] = mid[m] + bases[d][m] * kept
+                ns[y][m] = ns[y][m] + bases[d][m] * to_y
+                ew[x][m] = ew[x][m] + bases[d][m] * to_x
+        for m in range(5):
+            gsum[5 * w + m] = (
+                mid[m]
+                + jnp.where(sub > 0, roll(ns[0][m], 1, 0), 0.0)
+                + jnp.where(sub < 7, roll(ns[1][m], -1, 0), 0.0)
+                + jnp.where(lane > 0, roll(ew[0][m], 1, 1), 0.0)
+                + jnp.where(lane < 127, roll(ew[1][m], -1, 1), 0.0)
+            )
+            for i, out in enumerate((ns[0][m], ns[1][m], ew[0][m], ew[1][m])):
+                sums[i, 5 * w + m] = out
+
+    for g in range(n_sum):
+        hrow[0, g:g + 1, :] = sums[0, g, 7:8, :]
+        hrow[1, g:g + 1, :] = sums[1, g, 0:1, :]
+    to_east, to_west = zero, zero
+    for g in range(n_sum):
+        to_east = jnp.where(lane == g, roll(sums[2, g], g - 127, 1), to_east)
+        to_west = jnp.where(lane == g, roll(sums[3, g], g, 1), to_west)
+    hcol[0] = to_east
+    hcol[1] = to_west
+
+    def pack_rows(tiles, ref):
+        for p in range(len(tiles) // 2):
+            a, b = tiles[2 * p], tiles[2 * p + 1]
+            ref[0, p] = jnp.where(sub >= 4, b, roll(a, 4, 0))
+            ref[1, p] = jnp.where(sub < 4, a, roll(b, 4, 0))
+
+    def pack_cols(tiles, ref):
+        to_east = jnp.zeros((8, 128), f32)
+        to_west = jnp.zeros((8, 128), f32)
+        for i, tile in enumerate(tiles):
+            here = (lane >= 4 * i) & (lane < 4 * i + 4)
+            to_east = jnp.where(here, roll(tile, 4 * i + 4, 1), to_east)
+            to_west = jnp.where(here, roll(tile, 4 * i, 1), to_west)
+        ref[0] = to_east
+        ref[1] = to_west
+
+    plain = [own[q * levels + p] for q in range(2) for p in range(1, levels)]
+    n_near = len(plain)
+    tiles = plain + [own[0], own[levels], edges[0], edges[1]]
+    pack_rows(tiles, rowpk)
+    pack_cols(tiles, colpk)
+
+    edge = jnp.where(north_ok, 0, 3) + jnp.where(south_ok, 0, 3)
+    pl.semaphore_wait(barrier, 9 - edge)
+    for ds, dy, dx in partners:
+        if ds == 0:
+            def say(dy=dy, dx=dx):
+                pl.semaphore_signal(ready, inc=1, device_id=target(0, dy, dx), device_id_type=MESH)
+            when_to(dy, say)
 
     messages = []
 
@@ -202,150 +252,114 @@
     def wait_send(i):
         when_to(messages[i][3], lambda: make(i).wait_send())
 
-    center = message(fld.at[0:2 * levels], oth, 1, 0, 0)
+    center = message(own, oth, 1, 0, 0)
+    rim_sums = [message(hrow.at[s], hrow_in.at[s], 0, 1 - 2 * s, 0) for s in range(2)]
+    rim_sums += [message(hcol.at[s], hcol_in.at[s], 0, 0, 1 - 2 * s) for s in range(2)]
     cols = [message(send_cols.at[s], recv_cols.at[s], 0, 0, 1 - 2 * s) for s in range(2)]
     rows = [
         [message(send_rows.at[s, c], recv_rows.at[s, c], 0, 1 - 2 * s, 0) for s in range(2)]
         for c in range(CHUNKS)
     ]
 
-    def edge_messages(row_src, row_dst, col_src, col_dst):
+    def edge_messages(ds, row_src, row_dst, col_src, col_dst, count):
         out = []
-        for ds in (1, 0):
-            for dy in (0, -1, 1):
-                for s in range(2):
-                    out.append(message(col_src.at[s], col_dst.at[ds, 1 + dy, s], ds, dy, 1 - 2 * s))
+        for dy in (-1, 1, 0):
             for s in range(2):
-                out.append(message(row_src.at[s], row_dst.at[ds, s], ds, 1 - 2 * s, 0))
+                out.append(message(col_src.at[s], col_dst.at[ds, 1 + dy, s], ds, dy, 1 - 2 * s))
+        for s in range(2):
+            out.append(
+                message(row_src.at[s, 0:count], row_dst.at[ds, s, 0:count], ds, 1 - 2 * s, 0)
+            )
         return out
 
-    field_edges = edge_messages(rowpk, rowpk_in, colpk, colpk_in)
-    for i in [center] + cols + rows[0]:
-        start(i)
-    for c in range(1, CHUNKS):
-        for i in rows[c]:
-            start(i)
-    for i in field_edges:
+    field_edges = edge_messages(0, rowpk, row_in, colpk, col_in, (2 * levels + 2) // 2)
+    for i in [center] + rim_sums + cols + sum(rows, []) + field_edges:
         start(i)
 
     @pl.when(jnp.logical_not(south_ok))
     def _():
         recv_rows[0] = jnp.zeros(recv_rows.shape[1:], f32)
+        hrow_in[0] = jnp.zeros(hrow_in.shape[1:], f32)
 
     @pl.when(jnp.logical_not(north_ok))
     def _():
         recv_rows[1] = jnp.zeros(recv_rows.shape[1:], f32)
-
-    quadrants = []
+        hrow_in[1] = jnp.zeros(hrow_in.shape[1:], f32)
+
+    for i in rim_sums:
+        wait_recv(i)
+    full = []
+    for g in range(n_sum):
+        full.append(
+            gsum[g]
+            + jnp.where(sub == 0, hrow_in[0, g:g + 1, :], 0.0)
+            + jnp.where(sub == 7, hrow_in[1, g:g + 1, :], 0.0)
+            + jnp.where(lane == 0, roll(hcol_in[0], -g, 1), 0.0)
+            + jnp.where(lane == 127, roll(hcol_in[1], 127 - g, 1), 0.0)
+        )
+    pl.semaphore_wait(ready, 8 - edge)
+    cross = edge_messages(1, rowpk, row_in, colpk, col_in, n_near // 2)
+    for i in cross:
+        start(i)
+    field_edges += cross
+
+    wait_recv(center)
+    su = jnp.where(first, own[0], oth[0])
+    sv = jnp.where(first, own[levels], oth[levels])
+    parts = []
+    for w in range(2):
+        c, s, cc, cs, ss = full[5 * w:5 * w + 5]
+        parts.append(sea * (c + CURRENT_GAIN * (su * cc + sv * cs)))
+        parts.append(sea * (s + CURRENT_GAIN * (su * cs + sv * ss)))
+
+    for i in range(4):
+        cpl[i] = parts[i]
+    pack_rows(parts, rowc)
+    pack_cols(parts, colc)
+    coupling = []
+    coupling += edge_messages(1, rowc, rowc_in, colc, colc_in, 2)
+    coupling += [message(cpl, cplo, 1, 0, 0)]
+    coupling += edge_messages(0, rowc, rowc_in, colc, colc_in, 2)
+    for i in coupling:
+        start(i)
+
     for d in range(dirs):
-        kind = (cosines[d] > 0, sines[d] > 0)
-        if quadrants and quadrants[-1][0] == kind:
-            quadrants[-1][2] += 1
-        else:
-            quadrants.append([kind, d, 1])
-
-    def wave(chunk):
-        f0 = chunk * per_chunk
-        speeds = [jnp.full((8, 128), courant[f0 + i], f32) for i in range(per_chunk)]
-        firsts = [jnp.full((8, 128), stokes[f0 + i], f32) for i in range(per_chunk)]
-        seconds = [jnp.full((8, 128), stress[f0 + i], f32) for i in range(per_chunk)]
-        for (to_east, to_north), d0, count in quadrants:
-            group = max(g for g in range(1, 4) if count % g == 0)
-            rim = 0 if to_north else 1
-            row0 = (north_dirs if to_north else south_dirs)[0]
-
-            def body(step, _):
-                for n in range(group):
-                    d = d0 + step * group + n
-                    along_x, along_y = table[0, d], table[1, d]
-                    if chunk == 0:
-                        a1 = jnp.zeros((8, 128), f32)
-                        a2 = jnp.zeros((8, 128), f32)
-                    else:
-                        a1, a2 = acc[0, d], acc[1, d]
-                    for fi in range(per_chunk):
-                        at = pl.ds(pl.multiple_of((f0 + fi) * dirs * 8 + d * 8, 8), 8)
-                        tile = spec[at, :]
-                        beside = roll(tile, 1 if to_east else -1, 1)
-                        row = recv_rows[rim, chunk, pl.ds(fi * half + d - row0, 1), :]
-                        if to_north:
-                            along = jnp.where(sub == 0, row, roll(tile, 1, 0))
-                        else:
-                            along = jnp.where(sub == 7, row, roll(tile, -1, 0))
-                        change = along_x * (beside - tile) + along_y * (along - tile)
-                        moved = tile + speeds[fi] * change
-                        out_spec[at, :] = moved
-                        a1 = a1 + firsts[fi] * moved
-                        a2 = a2 + seconds[fi] * moved
-                    acc[0, d] = a1
-                    acc[1, d] = a2
-                return 0
-
-            lax.fori_loop(0, count // group, body, 0)
+        dop[d] = sea * (1.0 + CURRENT_GAIN * (su * cosines[d] + sv * sines[d]))
+    for i in cols:
+        wait_recv(i)
+
+    def wave(chunk, fi, _):
+        f = chunk * per_chunk + fi
+        base = f * (dirs * 8)
+        speed = jnp.full((8, 128), courant[f], f32)
+        g = f // per_group
+        m = f - g * per_group
+        back = lax.rem(128 - half * m, 128)
+        from_west = pltpu.roll(recv_cols[0, g], back, 1)
+        from_east = pltpu.roll(recv_cols[1, g], back, 1)
+        for d in range(dirs):
+            at = pl.ds(pl.multiple_of(base + d * 8, 8), 8)
+            tile = spec[at, :]
+            if cosines[d] > 0:
+                j = east_dirs.index(d)
+                beside = jnp.where(lane == 0, roll(from_west, -j, 1), roll(tile, 1, 1))
+            else:
+                j = west_dirs.index(d)
+                beside = jnp.where(lane == 127, roll(from_east, 127 - j, 1), roll(tile, -1, 1))
+            if sines[d] > 0:
+                row = recv_rows[0, chunk, pl.ds(fi * half + north_dirs.index(d), 1), :]
+                along = jnp.where(sub == 0, row, roll(tile, 1, 0))
+            else:
+                row = recv_rows[1, chunk, pl.ds(fi * half + south_dirs.index(d), 1), :]
+                along = jnp.where(sub == 7, row, roll(tile, -1, 0))
+            change = abs(cosines[d]) * (beside - tile) + abs(sines[d]) * (along - tile)
+            out_spec[at, :] = (tile + speed * change) * dop[d]
+        return 0
 
     for c in range(CHUNKS):
         for i in rows[c]:
             wait_recv(i)
-        wave(c)
-
-    wait_recv(center)
-    first = sec == 0
-    su = jnp.where(first, fld[0], oth[0])
-    sv = jnp.where(first, fld[levels], oth[levels])
-    sums = [jnp.zeros((8, 128), f32)] * 4
-    for d in range(dirs):
-        factor = sea * (1.0 + CURRENT_GAIN * (su * cosines[d] + sv * sines[d]))
-        dop[d] = factor
-        a1, a2 = factor * acc[0, d], factor * acc[1, d]
-        sums[0] = sums[0] + cosines[d] * a1
-        sums[1] = sums[1] + sines[d] * a1
-        sums[2] = sums[2] + cosines[d] * a2
-        sums[3] = sums[3] + sines[d] * a2
-
-    for i in cols:
-        wait_recv(i)
-    for side in range(2):
-        at = 0 if side == 0 else 127
-        cos_l, sin_l = pats[3 * groups + 2 * side], pats[3 * groups + 2 * side + 1]
-        wide = lambda x: jnp.broadcast_to(x[:, at:at + 1], (8, 128))
-        factor = wide(sea) * (1.0 + CURRENT_GAIN * (wide(su) * cos_l + wide(sv) * sin_l))
-        s1 = jnp.zeros((8, 128), f32)
-        s2 = jnp.zeros((8, 128), f32)
-        for g in range(groups):
-            rim = pats[g] * jnp.abs(cos_l) * (recv_cols[side, g] - send_cols[side, g])
-            rims[side, g] = rim
-            s1 = s1 + pats[groups + g] * (rim * factor)
-            s2 = s2 + pats[2 * groups + g] * (rim * factor)
-        for n, part in enumerate((s1 * cos_l, s1 * sin_l, s2 * cos_l, s2 * sin_l)):
-            extra = jnp.broadcast_to(jnp.sum(part, axis=1, keepdims=True), (8, 128))
-            sums[n] = sums[n] + jnp.where(lane == at, extra, 0.0)
-
-    for i in range(4):
-        cpl[i] = sums[i]
-    pack_rows(sums, rowc)
-    pack_cols(sums, colc)
-    middle = message(cpl, cplo, 1, 0, 0)
-    coupling_edges = [middle] + edge_messages(rowc, rowc_in, colc, colc_in)
-    for i in coupling_edges:
-        start(i)
-
-    def finish(f, _):
-        base = f * (dirs * 8)
-        g = f // per_group
-        m = f - g * per_group
-        back = lax.rem(128 - half * m, 128)
-        from_west = pltpu.roll(rims[0, g], back, 1)
-        from_east = pltpu.roll(rims[1, g], back, 1)
-        for d in range(dirs):
-            at = pl.ds(pl.multiple_of(base + d * 8, 8), 8)
-            if cosines[d] > 0:
-                extra = jnp.where(lane == 0, roll(from_west, -east_dirs.index(d), 1), 0.0)
-            else:
-                extra = jnp.where(lane == 127, roll(from_east, 127 - west_dirs.index(d), 1), 0.0)
-            out_spec[at, :] = (out_spec[at, :] + extra) * dop[d]
-        return 0
-
-    lax.fori_loop(0, freqs, finish, 0)
+        lax.fori_loop(0, per_chunk, functools.partial(wave, c), 0)
 
     inside = jnp.where(sub < 4, north_ok.astype(jnp.int32), south_ok.astype(jnp.int32)) != 0
     zero = jnp.zeros((8, 128), f32)
@@ -386,16 +400,21 @@
         ref[index + (slice(8, 16), slice(128, 256))] = ghost_lanes(corner[0], corner[1], i)
 
     for r in range(2):
-        got = packs(rowpk_in, colpk_in, r, n_fld)
+        got = packs(row_in, col_in, r, 2 * levels + 2 if r == 0 else n_near)
         for q in range(2):
-            for k in range(levels):
-                i = q * levels + k
-                own = fld[i] if r == 0 else oth[i]
-                position = r * levels + jnp.where(first, k, levels - 1 - k)
-                place(ext, (q, position), own, got, i)
+            for p in range(levels):
+                tile = (own if r == 0 else oth)[q * levels + p]
+                at = (q, p if r == 0 else 2 * levels - 1 - p)
+                if p > 0:
+                    place(ext, at, tile, got, q * (levels - 1) + p - 1)
+                elif r == 0:
+                    place(ext, at, tile, got, n_near + q)
+                else:
+                    ext[at] = jnp.zeros((16, 256), f32)
+                    ext[at + (slice(0, 8), slice(0, 128))] = tile
         if r == 0:
-            place(aux, (0,), fld[2 * levels], got, 2 * levels)
-            place(aux, (1,), fld[2 * levels + 1], got, 2 * levels + 1)
+            for n in range(2):
+                place(aux, (n,), edges[n], got, n_near + 2 + n)
 
     big_sub = lax.broadcasted_iota(jnp.int32, (16, 256), 0)
     row_index = jnp.where(big_sub < 12, big_sub, big_sub - 16) + lat * 8
@@ -410,7 +429,7 @@
     ocean_level(ext, ext2, aux, None, first, total, 0)
     lax.fori_loop(1, total - 1, at_level, 0)
 
-    for i in coupling_edges:
+    for i in coupling:
         wait_recv(i)
     got = [packs(rowc_in, colc_in, r, 4) for r in range(2)]
     both = jax.tree.map(lambda a, b: a + b, got[0], got[1])
@@ -491,11 +510,10 @@
     half = dirs // 2
     rows = -(-freqs // CHUNKS * half // 8) * 8
     groups = -(-freqs // (128 // half))
-    n_fld = 2 * levels + 2
     tile = (8, 128)
     vmem = lambda *shape: pltpu.VMEM(shape, f32)
     any_spec = pl.BlockSpec(memory_space=pl.ANY)
-    n_msg = 3 + 2 * CHUNKS + 16 + 17
+    n_msg = 7 + 2 * CHUNKS + 16 + 17
     big = (2, 2 * levels, 16, 256)
     vmem_spec = pl.BlockSpec(memory_space=pltpu.VMEM)
     results = pl.pallas_call(
@@ -510,17 +528,18 @@
             pltpu.SMEM((2, dirs), f32),
             vmem(2, CHUNKS, rows, 128), vmem(2, CHUNKS, rows, 128),
             vmem(2, groups, *tile), vmem(2, groups, *tile),
-            vmem(n_fld, *tile), vmem(2 * levels, *tile),
-            vmem(2, n_fld // 2, *tile), vmem(2, 2, n_fld // 2, *tile),
+            vmem(2 * levels, *tile), vmem(2 * levels, *tile), vmem(2, *tile),
+            vmem(2, levels + 1, *tile), vmem(2, 2, levels + 1, *tile),
             vmem(2, *tile), vmem(2, 3, 2, *tile),
             vmem(4, *tile), vmem(4, *tile),
             vmem(2, 2, *tile), vmem(2, 2, 2, *tile),
             vmem(2, *tile), vmem(2, 3, 2, *tile),
-            vmem(dirs, *tile), vmem(2, dirs, *tile), vmem(*big),
-            vmem(3 * groups + 4, *tile), vmem(2, groups, *tile),
+            vmem(dirs, *tile), vmem(4, dirs, *tile), vmem(10, *tile), vmem(4, 10, *tile),
+            vmem(2, 16, 128), vmem(2, 16, 128), vmem(2, *tile), vmem(2, *tile), vmem(*big),
             pltpu.SemaphoreType.DMA((7,)),
             pltpu.SemaphoreType.DMA((n_msg,)),
             pltpu.SemaphoreType.DMA((n_msg,)),
+            pltpu.SemaphoreType.REGULAR,
         ],
         compiler_params=pltpu.CompilerParams(collective_id=0, has_side_effects=True),
         name="window",

time: 28.6 us -> 28.7 us (level)
  the two profiles are of different devices: /device:TPU:1 before, /device:TPU:2 now
where the time goes in v3:
time: 28.7 us; the launch traced here: 28.6 us
  Pallas kernels  27.9 us (97%)
  between operations  0.64 us (2%)
    pallas_call x1, Pallas kernels, shards(): pl.pallas_call(functools.partial(kernel, freqs, dirs, levels, lats, lons)...  26.4 us
    pallas_call x1, Pallas kernels, shards(): pl.pallas_call(functools.partial(emit, levels), out_shape=(jax.ShapeDtype...  1.59 us

profile of v3, /device:TPU:2, one launch (start us, length us, event | category | flops | bytes accessed | tf_op | source)
XLA Modules:
  0.0 28.6 jit_solution(8123649442532000466)
XLA Ops:
  0.6 26.4 %window.1 = (f32[5184,128]{1,0:T(8,128)S(1)}, f32[2,8,16,256]{3,2,1,0:T(8,128)S(1)}, f32[3,16,256]{2,1,0:T(8,128)S(1)}, f32[4,16,256]{2,1,0:T(8,128)S(1)}) custom-call(f32[5184,128]{1,0:T(8,128)} %bitcast.2, f32[2,4,8,128]{3,2,1,0:T(8,128)} %cur_hbm.1, s32[8,128]{1,0:T(8,128)} %mask_hbm.1, f32[8,128]{1,0:T(8,128)} %diff_hbm.1, f32[18]{0:T(128)} %courant_hbm.1, ...), custom_call_target="tpu_custom_call" | custom-call | tf_op jit(solution)/shard_map/window/pallas_call | solution.py:519
  27.0 1.6 %emit.1 = (f32[5184,128]{1,0:T(8,128)}, f32[2,4,8,128]{3,2,1,0:T(8,128)}) custom-call(f32[5184,128]{1,0:T(8,128)S(1)} %get-tuple-element.8.spec, f32[2,8,16,256]{3,2,1,0:T(8,128)S(1)} %get-tuple-element.9.ext2, f32[3,16,256]{2,1,0:T(8,128)S(1)} %get-tuple-element.10.aux, f32[4,16,256]{2,1,0:T(8,128)S(1)} %get-tuple-element.11.frc), custom_call_target="tpu_custom_call" | custom-call | tf_op jit(solution)/shard_map/emit/pallas_call | solution.py:548

commit v4 on v3

--- a/solution.py
+++ b/solution.py
@@ -32,13 +32,13 @@
 def kernel(
     freqs, dirs, levels, lats, lons,
     spec_hbm, cur_hbm, mask_hbm, diff_hbm, courant_hbm, stokes_hbm, stress_hbm,
-    out_spec, ext2, aux, frc,
+    out_spec, ext, aux, frc,
     spec, curv, maskv, diffv, courant, stokes, stress, table,
     send_rows, recv_rows, send_cols, recv_cols,
     own, oth, edges, rowpk, row_in, colpk, col_in,
-    cpl, cplo, rowc, rowc_in, colc, colc_in,
-    dop, acc, gsum, sums, hrow, hrow_in, hcol, hcol_in, ext,
-    local_sem, send_sem, recv_sem, ready,
+    pos, pos_in, rowc, rowc_in, colc, colc_in,
+    dop, acc, sums,
+    local_sem, send_sem, recv_sem,
 ):
     sec, lat, lon = lax.axis_index("sec"), lax.axis_index("lat"), lax.axis_index("lon")
     north_ok, south_ok = lat < lats - 1, lat > 0
@@ -180,7 +180,7 @@
                 ns[y][m] = ns[y][m] + bases[d][m] * to_y
                 ew[x][m] = ew[x][m] + bases[d][m] * to_x
         for m in range(5):
-            gsum[5 * w + m] = (
+            pos[5 * w + m] = (
                 mid[m]
                 + jnp.where(sub > 0, roll(ns[0][m], 1, 0), 0.0)
                 + jnp.where(sub < 7, roll(ns[1][m], -1, 0), 0.0)
@@ -190,45 +190,37 @@
             for i, out in enumerate((ns[0][m], ns[1][m], ew[0][m], ew[1][m])):
                 sums[i, 5 * w + m] = out
 
+    rims_e_w = zero
     for g in range(n_sum):
-        hrow[0, g:g + 1, :] = sums[0, g, 7:8, :]
-        hrow[1, g:g + 1, :] = sums[1, g, 0:1, :]
-    to_east, to_west = zero, zero
-    for g in range(n_sum):
-        to_east = jnp.where(lane == g, roll(sums[2, g], g - 127, 1), to_east)
-        to_west = jnp.where(lane == g, roll(sums[3, g], g, 1), to_west)
-    hcol[0] = to_east
-    hcol[1] = to_west
+        for side, row in ((0, 7), (1, 0)):
+            at = 2 * g + side
+            pos[n_sum + at // 8, at % 8:at % 8 + 1, :] = sums[side, g, row:row + 1, :]
+        rims_e_w = jnp.where(lane == g, roll(sums[2, g], g - 127, 1), rims_e_w)
+        rims_e_w = jnp.where(lane == n_sum + g, roll(sums[3, g], n_sum + g, 1), rims_e_w)
+    n_pos = n_sum + -(-2 * n_sum // 8)
+    pos[n_pos] = rims_e_w
 
     def pack_rows(tiles, ref):
         for p in range(len(tiles) // 2):
-            a, b = tiles[2 * p], tiles[2 * p + 1]
-            ref[0, p] = jnp.where(sub >= 4, b, roll(a, 4, 0))
-            ref[1, p] = jnp.where(sub < 4, a, roll(b, 4, 0))
+            (a_up, a_down), (b_up, b_down) = tiles[2 * p], tiles[2 * p + 1]
+            ref[0, p] = jnp.where(sub >= 4, b_up, roll(a_up, 4, 0))
+            ref[1, p] = jnp.where(sub < 4, a_down, roll(b_down, 4, 0))
 
     def pack_cols(tiles, ref):
-        to_east = jnp.zeros((8, 128), f32)
-        to_west = jnp.zeros((8, 128), f32)
-        for i, tile in enumerate(tiles):
+        to_east, to_west = zero, zero
+        for i, (te, tw) in enumerate(tiles):
             here = (lane >= 4 * i) & (lane < 4 * i + 4)
-            to_east = jnp.where(here, roll(tile, 4 * i + 4, 1), to_east)
-            to_west = jnp.where(here, roll(tile, 4 * i, 1), to_west)
+            to_east = jnp.where(here, roll(te, 4 * i + 4, 1), to_east)
+            to_west = jnp.where(here, roll(tw, 4 * i, 1), to_west)
         ref[0] = to_east
         ref[1] = to_west
 
-    plain = [own[q * levels + p] for q in range(2) for p in range(1, levels)]
-    n_near = len(plain)
-    tiles = plain + [own[0], own[levels], edges[0], edges[1]]
-    pack_rows(tiles, rowpk)
-    pack_cols(tiles, colpk)
+    same = [(t, t) for t in [own[i] for i in range(n_fld)] + [edges[0], edges[1]]]
+    pack_rows(same, rowpk)
+    pack_cols(same, colpk)
 
     edge = jnp.where(north_ok, 0, 3) + jnp.where(south_ok, 0, 3)
     pl.semaphore_wait(barrier, 9 - edge)
-    for ds, dy, dx in partners:
-        if ds == 0:
-            def say(dy=dy, dx=dx):
-                pl.semaphore_signal(ready, inc=1, device_id=target(0, dy, dx), device_id_type=MESH)
-            when_to(dy, say)
 
     messages = []
 
@@ -252,79 +244,40 @@
     def wait_send(i):
         when_to(messages[i][3], lambda: make(i).wait_send())
 
-    center = message(own, oth, 1, 0, 0)
-    rim_sums = [message(hrow.at[s], hrow_in.at[s], 0, 1 - 2 * s, 0) for s in range(2)]
-    rim_sums += [message(hcol.at[s], hcol_in.at[s], 0, 0, 1 - 2 * s) for s in range(2)]
+    center = [message(pos, pos_in, 1, 0, 0), message(own, oth, 1, 0, 0)]
     cols = [message(send_cols.at[s], recv_cols.at[s], 0, 0, 1 - 2 * s) for s in range(2)]
     rows = [
         [message(send_rows.at[s, c], recv_rows.at[s, c], 0, 1 - 2 * s, 0) for s in range(2)]
         for c in range(CHUNKS)
     ]
 
-    def edge_messages(ds, row_src, row_dst, col_src, col_dst, count):
+    def edge_messages(row_src, row_dst, col_src, col_dst):
         out = []
         for dy in (-1, 1, 0):
             for s in range(2):
-                out.append(message(col_src.at[s], col_dst.at[ds, 1 + dy, s], ds, dy, 1 - 2 * s))
+                out.append(message(col_src(dy).at[s], col_dst.at[1 + dy, s], 0, dy, 1 - 2 * s))
         for s in range(2):
-            out.append(
-                message(row_src.at[s, 0:count], row_dst.at[ds, s, 0:count], ds, 1 - 2 * s, 0)
-            )
+            out.append(message(row_src.at[s], row_dst.at[s], 0, 1 - 2 * s, 0))
         return out
 
-    field_edges = edge_messages(0, rowpk, row_in, colpk, col_in, (2 * levels + 2) // 2)
-    for i in [center] + rim_sums + cols + sum(rows, []) + field_edges:
+    field_edges = edge_messages(rowpk, row_in, lambda dy: colpk, col_in)
+    for i in center + cols + sum(rows, []) + field_edges:
         start(i)
 
     @pl.when(jnp.logical_not(south_ok))
     def _():
         recv_rows[0] = jnp.zeros(recv_rows.shape[1:], f32)
-        hrow_in[0] = jnp.zeros(hrow_in.shape[1:], f32)
+        for rows_in, cols_in in ((row_in, col_in), (rowc_in, colc_in)):
+            rows_in[0] = jnp.zeros(rows_in.shape[1:], f32)
+            cols_in[2] = jnp.zeros(cols_in.shape[1:], f32)
 
     @pl.when(jnp.logical_not(north_ok))
     def _():
         recv_rows[1] = jnp.zeros(recv_rows.shape[1:], f32)
-        hrow_in[1] = jnp.zeros(hrow_in.shape[1:], f32)
-
-    for i in rim_sums:
-        wait_recv(i)
-    full = []
-    for g in range(n_sum):
-        full.append(
-            gsum[g]
-            + jnp.where(sub == 0, hrow_in[0, g:g + 1, :], 0.0)
-            + jnp.where(sub == 7, hrow_in[1, g:g + 1, :], 0.0)
-            + jnp.where(lane == 0, roll(hcol_in[0], -g, 1), 0.0)
-            + jnp.where(lane == 127, roll(hcol_in[1], 127 - g, 1), 0.0)
-        )
-    pl.semaphore_wait(ready, 8 - edge)
-    cross = edge_messages(1, rowpk, row_in, colpk, col_in, n_near // 2)
-    for i in cross:
-        start(i)
-    field_edges += cross
-
-    wait_recv(center)
-    su = jnp.where(first, own[0], oth[0])
-    sv = jnp.where(first, own[levels], oth[levels])
-    parts = []
-    for w in range(2):
-        c, s, cc, cs, ss = full[5 * w:5 * w + 5]
-        parts.append(sea * (c + CURRENT_GAIN * (su * cc + sv * cs)))
-        parts.append(sea * (s + CURRENT_GAIN * (su * cs + sv * ss)))
-
-    for i in range(4):
-        cpl[i] = parts[i]
-    pack_rows(parts, rowc)
-    pack_cols(parts, colc)
-    coupling = []
-    coupling += edge_messages(1, rowc, rowc_in, colc, colc_in, 2)
-    coupling += [message(cpl, cplo, 1, 0, 0)]
-    coupling += edge_messages(0, rowc, rowc_in, colc, colc_in, 2)
-    for i in coupling:
-        start(i)
-
-    for d in range(dirs):
-        dop[d] = sea * (1.0 + CURRENT_GAIN * (su * cosines[d] + sv * sines[d]))
+        for rows_in, cols_in in ((row_in, col_in), (rowc_in, colc_in)):
+            rows_in[1] = jnp.zeros(rows_in.shape[1:], f32)
+            cols_in[0] = jnp.zeros(cols_in.shape[1:], f32)
+
     for i in cols:
         wait_recv(i)
 
@@ -353,88 +306,156 @@
                 row = recv_rows[1, chunk, pl.ds(fi * half + south_dirs.index(d), 1), :]
                 along = jnp.where(sub == 7, row, roll(tile, -1, 0))
             change = abs(cosines[d]) * (beside - tile) + abs(sines[d]) * (along - tile)
-            out_spec[at, :] = (tile + speed * change) * dop[d]
+            out_spec[at, :] = tile + speed * change
         return 0
 
     for c in range(CHUNKS):
         for i in rows[c]:
             wait_recv(i)
-        lax.fori_loop(0, per_chunk, functools.partial(wave, c), 0)
-
-    inside = jnp.where(sub < 4, north_ok.astype(jnp.int32), south_ok.astype(jnp.int32)) != 0
-    zero = jnp.zeros((8, 128), f32)
-
-    def ghost_rows(from_south, from_north, i):
+        if c < CHUNKS - 1:
+            lax.fori_loop(0, per_chunk, functools.partial(wave, c), 0)
+
+    for i in center:
+        wait_recv(i)
+    for i in range(n_pos + 1):
+        pos_in[i] = pos_in[i] + pos[i]
+    rims = pos_in[n_pos]
+
+    def rim_row(g, side):
+        at = 2 * g + side
+        return pos_in[n_sum + at // 8, at % 8:at % 8 + 1, :]
+
+    def rim_col(g, side, at):
+        return roll(rims, at - n_sum * side - g, 1)
+
+    packed = [(oth[i], oth[i]) for i in range(n_fld)]
+    by_dy = {dy: list(packed) for dy in (-1, 0, 1)}
+    for g in range(n_sum):
+        tile = pos_in[g]
+        to_e, to_w = rim_col(g, 0, 127), rim_col(g, 1, 0)
+        up = jnp.where(sub == 7, rim_row(g, 0), roll(tile, -1, 0))
+        down = jnp.where(sub == 0, rim_row(g, 1), roll(tile, 1, 0))
+        packed.append((up, down))
+        pick = lambda t, e, w: (
+            jnp.where(lane == 127, e, roll(t, -1, 1)), jnp.where(lane == 0, w, roll(t, 1, 1))
+        )
+        by_dy[0].append(pick(tile, to_e, to_w))
+        by_dy[1].append(pick(up, *(jnp.where(sub == 7, 0.0, roll(t, -1, 0)) for t in (to_e, to_w))))
+        by_dy[-1].append(pick(down, *(jnp.where(sub == 0, 0.0, roll(t, 1, 0)) for t in (to_e, to_w))))
+    pack_rows(packed, rowc)
+    for s in range(2):
+        rowc[s, len(packed) // 2] = rims
+    for g in range(n_sum):
+        tile = jnp.where(sub == 7, rim_row(g, 0), jnp.where(sub == 0, rim_row(g, 1), 0.0))
+        by_dy[0].append((roll(tile, -1, 1), roll(tile, 1, 1)))
+    for dy in by_dy:
+        pack_cols(by_dy[dy], colc.at[1 + dy])
+    sum_edges = edge_messages(rowc, rowc_in, lambda dy: colc.at[1 + dy], colc_in)
+    for i in sum_edges:
+        start(i)
+
+    lax.fori_loop(0, per_chunk, functools.partial(wave, CHUNKS - 1), 0)
+    su = jnp.where(first, own[0], oth[0])
+    sv = jnp.where(first, own[levels], oth[levels])
+    for d in range(dirs):
+        dop[d] = sea * (1.0 + CURRENT_GAIN * (su * cosines[d] + sv * sines[d]))
+
+    def scale(f, _):
+        for d in range(dirs):
+            at = pl.ds(pl.multiple_of(f * (dirs * 8) + d * 8, 8), 8)
+            out_spec[at, :] = out_spec[at, :] * dop[d]
+        return 0
+
+    lax.fori_loop(0, freqs, scale, 0)
+
+    for i in field_edges:
+        wait_recv(i)
+
+    def put(ref, index, quads):
+        for n, (r, l) in enumerate(((0, 0), (0, 128), (8, 0), (8, 128))):
+            ref[index + (slice(r, r + 8), slice(l, l + 128))] = quads[n]
+
+    def ghosts(rows_in, cols_in, i):
+        def lanes(dy):
+            return jnp.where(
+                lane < 4,
+                roll(cols_in[1 + dy, 1], -4 * i, 1),
+                jnp.where(lane >= 124, roll(cols_in[1 + dy, 0], 124 - 4 * i, 1), 0.0),
+            )
+
         p = i // 2
         if i % 2 == 0:
-            low, high = roll(from_south[p], 4, 0), from_north[p]
+            low, high = roll(rows_in[0, p], 4, 0), rows_in[1, p]
         else:
-            low, high = from_south[p], roll(from_north[p], 4, 0)
-        return jnp.where(inside, jnp.where(sub < 4, high, low), zero)
-
-    def ghost_lanes(from_west, from_east, i):
-        return jnp.where(
-            lane < 4,
-            roll(from_east, -4 * i, 1),
-            jnp.where(lane >= 124, roll(from_west, 124 - 4 * i, 1), zero),
-        )
-
-    for i in field_edges:
-        wait_recv(i)
-
-    def packs(rows_in, cols_in, r, count):
-        from_south = [rows_in[r, 0, p] for p in range(count // 2)]
-        from_north = [rows_in[r, 1, p] for p in range(count // 2)]
-        side = [cols_in[r, 1, s] for s in range(2)]
-        corner = [
-            jnp.where(inside, jnp.where(sub < 4, cols_in[r, 0, s], cols_in[r, 2, s]), zero)
-            for s in range(2)
-        ]
-        return from_south, from_north, side, corner
-
-    def place(ref, index, own, got, i):
-        from_south, from_north, side, corner = got
-        ref[index + (slice(0, 8), slice(0, 128))] = own
-        ref[index + (slice(0, 8), slice(128, 256))] = ghost_lanes(side[0], side[1], i)
-        ref[index + (slice(8, 16), slice(0, 128))] = ghost_rows(from_south, from_north, i)
-        ref[index + (slice(8, 16), slice(128, 256))] = ghost_lanes(corner[0], corner[1], i)
-
-    for r in range(2):
-        got = packs(row_in, col_in, r, 2 * levels + 2 if r == 0 else n_near)
-        for q in range(2):
-            for p in range(levels):
-                tile = (own if r == 0 else oth)[q * levels + p]
-                at = (q, p if r == 0 else 2 * levels - 1 - p)
-                if p > 0:
-                    place(ext, at, tile, got, q * (levels - 1) + p - 1)
-                elif r == 0:
-                    place(ext, at, tile, got, n_near + q)
-                else:
-                    ext[at] = jnp.zeros((16, 256), f32)
-                    ext[at + (slice(0, 8), slice(0, 128))] = tile
-        if r == 0:
-            for n in range(2):
-                place(aux, (n,), edges[n], got, n_near + 2 + n)
+            low, high = rows_in[0, p], roll(rows_in[1, p], 4, 0)
+        corner = jnp.where(sub < 4, lanes(-1), lanes(1))
+        return lanes(0), jnp.where(sub < 4, high, low), corner
+
+    for q in range(2):
+        for p in range(levels):
+            i = q * levels + p
+            put(ext, (q, p), (own[i],) + ghosts(row_in, col_in, i))
+    for n in range(2):
+        put(aux, (n,), (edges[n],) + ghosts(row_in, col_in, n_fld + n))
 
     big_sub = lax.broadcasted_iota(jnp.int32, (16, 256), 0)
     row_index = jnp.where(big_sub < 12, big_sub, big_sub - 16) + lat * 8
     aux[2] = 0.05 + 0.1 * (row_index.astype(f32) + 0.5) / (8 * lats)
 
-    total = 2 * levels
-
-    def at_level(p, _):
-        ocean_level(ext, ext2, aux, None, first, total, p)
-        return 0
-
-    ocean_level(ext, ext2, aux, None, first, total, 0)
-    lax.fori_loop(1, total - 1, at_level, 0)
-
-    for i in coupling:
+    for i in sum_edges:
         wait_recv(i)
-    got = [packs(rowc_in, colc_in, r, 4) for r in range(2)]
-    both = jax.tree.map(lambda a, b: a + b, got[0], got[1])
-    for i in range(4):
-        place(frc, (i,), cpl[i] + cplo[i], both, i)
+    for q in range(2):
+        for p in range(levels):
+            i = q * levels + p
+            put(ext, (q, 2 * levels - 1 - p), (oth[i],) + ghosts(rowc_in, colc_in, i))
+
+    def lanes_of(dy, i):
+        from_w = roll(colc_in[1 + dy, 0], 125 - 4 * i, 1)
+        from_e = roll(colc_in[1 + dy, 1], -4 * i - 1, 1)
+        inner = jnp.where(lane == 0, from_w, jnp.where(lane == 127, from_e, 0.0))
+        outer = jnp.where(lane < 3, from_e, jnp.where(lane >= 125, from_w, 0.0))
+        return inner, outer
+
+    last = (n_fld + n_sum) // 2
+    far_rims = jnp.where(sub < 3, rowc_in[1, last], jnp.where(sub >= 5, rowc_in[0, last], 0.0))
+    total = []
+    for g in range(n_sum):
+        i = n_fld + g
+        p = i // 2
+        inner, outer = lanes_of(0, i)
+        low = roll(rowc_in[0, p], 5 if i % 2 == 0 else 1, 0)
+        high = roll(rowc_in[1, p], -1 if i % 2 == 0 else 3, 0)
+        s_inner, s_outer = (roll(t, 1, 0) for t in lanes_of(1, i))
+        n_inner, n_outer = (roll(t, -1, 0) for t in lanes_of(-1, i))
+        low, high = low + s_inner, high + n_inner
+        mine_out = jnp.where(
+            lane == 0, rim_col(g, 0, 0), jnp.where(lane == 127, rim_col(g, 1, 127), 0.0)
+        )
+        mine_rows = jnp.where(sub == 0, rim_row(g, 0), jnp.where(sub == 7, rim_row(g, 1), 0.0))
+        beside = lanes_of(0, n_fld + n_sum + g)[1]
+        corner = jnp.where(
+            sub == 0, roll(beside, 1, 0), jnp.where(sub == 7, roll(beside, -1, 0), 0.0)
+        ) + jnp.where(
+            lane == 0, roll(far_rims, -g, 1),
+            jnp.where(lane == 127, roll(far_rims, 127 - n_sum - g, 1), 0.0),
+        )
+        edge_rows = lambda a, b: jnp.where(sub == 0, a, jnp.where(sub == 7, b, 0.0))
+        out_rows = lambda a, b: jnp.where(sub < 3, b, jnp.where(sub >= 5, a, 0.0))
+        total.append((
+            pos_in[g] + inner + edge_rows(low, high),
+            mine_out + outer + edge_rows(s_outer, n_outer),
+            mine_rows + out_rows(low, high),
+            corner + out_rows(s_outer, n_outer),
+        ))
+    surface_at = jnp.where(first, 0, 2 * levels - 1)
+    for n, (r, l) in enumerate(((0, 0), (0, 128), (8, 0), (8, 128))):
+        at = (slice(r, r + 8), slice(l, l + 128))
+        su = CURRENT_GAIN * ext[(0, surface_at) + at]
+        sv = CURRENT_GAIN * ext[(1, surface_at) + at]
+        for w in range(2):
+            c, s, cc, cs, ss = (total[5 * w + m][n] for m in range(5))
+            frc[(2 * w,) + at] = aux[(0,) + at] * (c + su * cc + sv * cs)
+            frc[(2 * w + 1,) + at] = aux[(0,) + at] * (s + su * cs + sv * ss)
     for i in range(len(messages)):
         wait_send(i)
 
@@ -477,7 +498,7 @@
             dst[q, own] = (aux[0] * new[q])[0:8, 0:128]
 
 
-def emit(levels, spec, ext2, aux, frc, out_spec, out_cur, fa, fb, cur, sems):
+def emit(levels, spec, ext, aux, frc, out_spec, out_cur, fa, fb, cur, sems):
     part = spec.shape[0] // EMIT
     copies = []
     for i in range(EMIT):
@@ -487,15 +508,11 @@
         copy.start()
     first = lax.axis_index("sec") == 0
     total = 2 * levels
-    for p in range(total - 1):
-        force = forcing(aux, frc, first, total, p)
-        for q in range(2):
-            fa[q, p] = ext2[q, p] + aux[0] * force[q]
-    src, dst = fa, fb
-    for step in range(1, ITERS):
+    src, dst = ext, fa
+    for step in range(ITERS):
         for p in range(total - 1 - step):
             ocean_level(src, cur if step == ITERS - 1 else dst, aux, frc, first, total, p)
-        src, dst = dst, src
+        src, dst = dst, fb if dst is fa else fa
     last = pltpu.make_async_copy(cur, out_cur, sems.at[EMIT])
     last.start()
     for copy in copies:
@@ -513,7 +530,7 @@
     tile = (8, 128)
     vmem = lambda *shape: pltpu.VMEM(shape, f32)
     any_spec = pl.BlockSpec(memory_space=pl.ANY)
-    n_msg = 7 + 2 * CHUNKS + 16 + 17
+    n_msg = 4 + 2 * CHUNKS + 16
     big = (2, 2 * levels, 16, 256)
     vmem_spec = pl.BlockSpec(memory_space=pltpu.VMEM)
     results = pl.pallas_call(
@@ -529,17 +546,15 @@
             vmem(2, CHUNKS, rows, 128), vmem(2, CHUNKS, rows, 128),
             vmem(2, groups, *tile), vmem(2, groups, *tile),
             vmem(2 * levels, *tile), vmem(2 * levels, *tile), vmem(2, *tile),
-            vmem(2, levels + 1, *tile), vmem(2, 2, levels + 1, *tile),
-            vmem(2, *tile), vmem(2, 3, 2, *tile),
-            vmem(4, *tile), vmem(4, *tile),
-            vmem(2, 2, *tile), vmem(2, 2, 2, *tile),
-            vmem(2, *tile), vmem(2, 3, 2, *tile),
-            vmem(dirs, *tile), vmem(4, dirs, *tile), vmem(10, *tile), vmem(4, 10, *tile),
-            vmem(2, 16, 128), vmem(2, 16, 128), vmem(2, *tile), vmem(2, *tile), vmem(*big),
+            vmem(2, levels + 1, *tile), vmem(2, levels + 1, *tile),
+            vmem(2, *tile), vmem(3, 2, *tile),
+            vmem(14, *tile), vmem(14, *tile),
+            vmem(2, levels + 6, *tile), vmem(2, levels + 6, *tile),
+            vmem(3, 2, *tile), vmem(3, 2, *tile),
+            vmem(dirs, *tile), vmem(4, dirs, *tile), vmem(4, 10, *tile),
             pltpu.SemaphoreType.DMA((7,)),
             pltpu.SemaphoreType.DMA((n_msg,)),
             pltpu.SemaphoreType.DMA((n_msg,)),
-            pltpu.SemaphoreType.REGULAR,
         ],
         compiler_params=pltpu.CompilerParams(collective_id=0, has_side_effects=True),
         name="window",

time: 28.7 us -> 27.3 us (0.951)
  the two profiles are of different devices: /device:TPU:2 before, /device:TPU:1 now
where the time goes in v4:
time: 27.3 us; the launch traced here: 27.2 us
  Pallas kernels  26.5 us (97%)
  between operations  0.64 us (2%)
    pallas_call x1, Pallas kernels, shards(): pl.pallas_call(functools.partial(kernel, freqs, dirs, levels, lats, lons)...  25 us
    pallas_call x1, Pallas kernels, shards(): pl.pallas_call(functools.partial(emit, levels), out_shape=(jax.ShapeDtype...  1.55 us

profile of v4, /device:TPU:1, one launch (start us, length us, event | category | flops | bytes accessed | tf_op | source)
XLA Modules:
  0.0 27.2 jit_solution(5878019020571380973)
XLA Ops:
  0.6 25.0 %window.1 = (f32[5184,128]{1,0:T(8,128)S(1)}, f32[2,8,16,256]{3,2,1,0:T(8,128)S(1)}, f32[3,16,256]{2,1,0:T(8,128)S(1)}, f32[4,16,256]{2,1,0:T(8,128)S(1)}) custom-call(f32[5184,128]{1,0:T(8,128)} %bitcast.2, f32[2,4,8,128]{3,2,1,0:T(8,128)} %cur_hbm.1, s32[8,128]{1,0:T(8,128)} %mask_hbm.1, f32[8,128]{1,0:T(8,128)} %diff_hbm.1, f32[18]{0:T(128)} %courant_hbm.1, ...), custom_call_target="tpu_custom_call" | custom-call | tf_op jit(solution)/shard_map/window/pallas_call | solution.py:536
  25.6 1.5 %emit.1 = (f32[5184,128]{1,0:T(8,128)}, f32[2,4,8,128]{3,2,1,0:T(8,128)}) custom-call(f32[5184,128]{1,0:T(8,128)S(1)} %get-tuple-element.8.spec, f32[2,8,16,256]{3,2,1,0:T(8,128)S(1)} %get-tuple-element.9.ext, f32[3,16,256]{2,1,0:T(8,128)S(1)} %get-tuple-element.10.aux, f32[4,16,256]{2,1,0:T(8,128)S(1)} %get-tuple-element.11.frc), custom_call_target="tpu_custom_call" | custom-call | tf_op jit(solution)/shard_map/emit/pallas_call | solution.py:563

commit v5 on v4

--- a/solution.py
+++ b/solution.py
@@ -36,7 +36,7 @@
     spec, curv, maskv, diffv, courant, stokes, stress, table,
     send_rows, recv_rows, send_cols, recv_cols,
     own, oth, edges, rowpk, row_in, colpk, col_in,
-    pos, pos_in, rowc, rowc_in, colc, colc_in,
+    pos, pos_in, rowc, rowc_in, colc, colc_in, rowo, rowo_in, colo, colo_in,
     dop, acc, sums,
     local_sem, send_sem, recv_sem,
 ):
@@ -160,6 +160,7 @@
 
     lax.fori_loop(0, dirs // group, weigh, 0)
 
+    gsum = [None] * n_sum
     zero = jnp.zeros((8, 128), f32)
     bases = [
         (c, s, c * c, c * s, s * s) for c, s in zip(cosines, sines)
@@ -180,7 +181,7 @@
                 ns[y][m] = ns[y][m] + bases[d][m] * to_y
                 ew[x][m] = ew[x][m] + bases[d][m] * to_x
         for m in range(5):
-            pos[5 * w + m] = (
+            gsum[5 * w + m] = (
                 mid[m]
                 + jnp.where(sub > 0, roll(ns[0][m], 1, 0), 0.0)
                 + jnp.where(sub < 7, roll(ns[1][m], -1, 0), 0.0)
@@ -190,15 +191,29 @@
             for i, out in enumerate((ns[0][m], ns[1][m], ew[0][m], ew[1][m])):
                 sums[i, 5 * w + m] = out
 
+    half_sum = n_sum // 2
+    row_tiles = -(-2 * n_sum // 8)
+    first_rows = -(-2 * half_sum // 8)
+    n_first = 1 + first_rows + half_sum
+    n_pos = 1 + row_tiles + n_sum
+
+    def sum_at(g):
+        return 1 + first_rows + g if g < half_sum else n_pos - n_sum + g
+
+    def row_at(g, side):
+        at = 2 * g + side
+        tile = 1 + at // 8 if at // 8 < first_rows else n_first + at // 8 - first_rows
+        return tile, slice(at % 8, at % 8 + 1)
+
     rims_e_w = zero
     for g in range(n_sum):
         for side, row in ((0, 7), (1, 0)):
-            at = 2 * g + side
-            pos[n_sum + at // 8, at % 8:at % 8 + 1, :] = sums[side, g, row:row + 1, :]
+            tile_at, rows_at = row_at(g, side)
+            pos[tile_at, rows_at, :] = sums[side, g, row:row + 1, :]
         rims_e_w = jnp.where(lane == g, roll(sums[2, g], g - 127, 1), rims_e_w)
         rims_e_w = jnp.where(lane == n_sum + g, roll(sums[3, g], n_sum + g, 1), rims_e_w)
-    n_pos = n_sum + -(-2 * n_sum // 8)
-    pos[n_pos] = rims_e_w
+        pos[sum_at(g)] = gsum[g]
+    pos[0] = rims_e_w
 
     def pack_rows(tiles, ref):
         for p in range(len(tiles) // 2):
@@ -235,14 +250,27 @@
             device_id=target(ds, dy, dx), device_id_type=MESH,
         )
 
+    def make_short():
+        return pltpu.make_async_remote_copy(
+            src_ref=pos.at[0:n_first], dst_ref=pos_in.at[0:n_first], send_sem=send_sem.at[0],
+            recv_sem=recv_sem.at[0], device_id=target(1, 0, 0), device_id_type=MESH,
+        )
+
+    def act(i, sign, short, what):
+        if i == 0:
+            pl.when(short)(lambda: what(make_short()))
+            pl.when(jnp.logical_not(short))(lambda: what(make(i)))
+        else:
+            when_to(sign * messages[i][3], lambda: what(make(i)))
+
     def start(i):
-        when_to(messages[i][3], lambda: make(i).start())
+        act(i, 1, first, lambda copy: copy.start())
 
     def wait_recv(i):
-        when_to(-messages[i][3], lambda: make(i).wait_recv())
+        act(i, -1, jnp.logical_not(first), lambda copy: copy.wait_recv())
 
     def wait_send(i):
-        when_to(messages[i][3], lambda: make(i).wait_send())
+        act(i, 1, first, lambda copy: copy.wait_send())
 
     center = [message(pos, pos_in, 1, 0, 0), message(own, oth, 1, 0, 0)]
     cols = [message(send_cols.at[s], recv_cols.at[s], 0, 0, 1 - 2 * s) for s in range(2)]
@@ -264,17 +292,21 @@
     for i in center + cols + sum(rows, []) + field_edges:
         start(i)
 
+    @pl.when(jnp.logical_not(first))
+    def _():
+        pos_in[n_first:n_pos] = jnp.zeros((n_pos - n_first, 8, 128), f32)
+
     @pl.when(jnp.logical_not(south_ok))
     def _():
         recv_rows[0] = jnp.zeros(recv_rows.shape[1:], f32)
-        for rows_in, cols_in in ((row_in, col_in), (rowc_in, colc_in)):
+        for rows_in, cols_in in ((row_in, col_in), (rowc_in, colc_in), (rowo_in, colo_in)):
             rows_in[0] = jnp.zeros(rows_in.shape[1:], f32)
             cols_in[2] = jnp.zeros(cols_in.shape[1:], f32)
 
     @pl.when(jnp.logical_not(north_ok))
     def _():
         recv_rows[1] = jnp.zeros(recv_rows.shape[1:], f32)
-        for rows_in, cols_in in ((row_in, col_in), (rowc_in, colc_in)):
+        for rows_in, cols_in in ((row_in, col_in), (rowc_in, colc_in), (rowo_in, colo_in)):
             rows_in[1] = jnp.zeros(rows_in.shape[1:], f32)
             cols_in[0] = jnp.zeros(cols_in.shape[1:], f32)
 
@@ -315,23 +347,22 @@
         if c < CHUNKS - 1:
             lax.fori_loop(0, per_chunk, functools.partial(wave, c), 0)
 
-    for i in center:
-        wait_recv(i)
-    for i in range(n_pos + 1):
+    wait_recv(center[0])
+    for i in range(n_pos):
         pos_in[i] = pos_in[i] + pos[i]
-    rims = pos_in[n_pos]
+    rims = pos_in[0]
 
     def rim_row(g, side):
-        at = 2 * g + side
-        return pos_in[n_sum + at // 8, at % 8:at % 8 + 1, :]
+        tile_at, rows_at = row_at(g, side)
+        return pos_in[tile_at, rows_at, :]
 
     def rim_col(g, side, at):
         return roll(rims, at - n_sum * side - g, 1)
 
-    packed = [(oth[i], oth[i]) for i in range(n_fld)]
-    by_dy = {dy: list(packed) for dy in (-1, 0, 1)}
+    packed = []
+    by_dy = {dy: [] for dy in (-1, 0, 1)}
     for g in range(n_sum):
-        tile = pos_in[g]
+        tile = pos_in[sum_at(g)]
         to_e, to_w = rim_col(g, 0, 127), rim_col(g, 1, 0)
         up = jnp.where(sub == 7, rim_row(g, 0), roll(tile, -1, 0))
         down = jnp.where(sub == 0, rim_row(g, 1), roll(tile, 1, 0))
@@ -342,16 +373,27 @@
         by_dy[0].append(pick(tile, to_e, to_w))
         by_dy[1].append(pick(up, *(jnp.where(sub == 7, 0.0, roll(t, -1, 0)) for t in (to_e, to_w))))
         by_dy[-1].append(pick(down, *(jnp.where(sub == 0, 0.0, roll(t, 1, 0)) for t in (to_e, to_w))))
+    for g in range(n_sum):
+        tile = jnp.where(sub == 7, rim_row(g, 0), jnp.where(sub == 0, rim_row(g, 1), 0.0))
+        by_dy[0].append((roll(tile, -1, 1), roll(tile, 1, 1)))
+    sum_edges = edge_messages(rowc, rowc_in, lambda dy: colc.at[1 + dy], colc_in)
+    for n, dy in enumerate((-1, 1, 0)):
+        pack_cols(by_dy[dy], colc.at[1 + dy])
+        for i in sum_edges[2 * n:2 * n + 2]:
+            start(i)
     pack_rows(packed, rowc)
     for s in range(2):
         rowc[s, len(packed) // 2] = rims
-    for g in range(n_sum):
-        tile = jnp.where(sub == 7, rim_row(g, 0), jnp.where(sub == 0, rim_row(g, 1), 0.0))
-        by_dy[0].append((roll(tile, -1, 1), roll(tile, 1, 1)))
-    for dy in by_dy:
-        pack_cols(by_dy[dy], colc.at[1 + dy])
-    sum_edges = edge_messages(rowc, rowc_in, lambda dy: colc.at[1 + dy], colc_in)
-    for i in sum_edges:
+    for i in sum_edges[6:]:
+        start(i)
+    wait_recv(center[1])
+    fields = [(oth[i], oth[i]) for i in range(n_fld)]
+    oth_edges = edge_messages(rowo, rowo_in, lambda dy: colo, colo_in)
+    pack_cols(fields, colo)
+    for i in oth_edges[:6]:
+        start(i)
+    pack_rows(fields, rowo)
+    for i in oth_edges[6:]:
         start(i)
 
     lax.fori_loop(0, per_chunk, functools.partial(wave, CHUNKS - 1), 0)
@@ -404,10 +446,6 @@
 
     for i in sum_edges:
         wait_recv(i)
-    for q in range(2):
-        for p in range(levels):
-            i = q * levels + p
-            put(ext, (q, 2 * levels - 1 - p), (oth[i],) + ghosts(rowc_in, colc_in, i))
 
     def lanes_of(dy, i):
         from_w = roll(colc_in[1 + dy, 0], 125 - 4 * i, 1)
@@ -416,11 +454,11 @@
         outer = jnp.where(lane < 3, from_e, jnp.where(lane >= 125, from_w, 0.0))
         return inner, outer
 
-    last = (n_fld + n_sum) // 2
+    last = n_sum // 2
     far_rims = jnp.where(sub < 3, rowc_in[1, last], jnp.where(sub >= 5, rowc_in[0, last], 0.0))
     total = []
     for g in range(n_sum):
-        i = n_fld + g
+        i = g
         p = i // 2
         inner, outer = lanes_of(0, i)
         low = roll(rowc_in[0, p], 5 if i % 2 == 0 else 1, 0)
@@ -432,7 +470,7 @@
             lane == 0, rim_col(g, 0, 0), jnp.where(lane == 127, rim_col(g, 1, 127), 0.0)
         )
         mine_rows = jnp.where(sub == 0, rim_row(g, 0), jnp.where(sub == 7, rim_row(g, 1), 0.0))
-        beside = lanes_of(0, n_fld + n_sum + g)[1]
+        beside = lanes_of(0, n_sum + g)[1]
         corner = jnp.where(
             sub == 0, roll(beside, 1, 0), jnp.where(sub == 7, roll(beside, -1, 0), 0.0)
         ) + jnp.where(
@@ -442,11 +480,17 @@
         edge_rows = lambda a, b: jnp.where(sub == 0, a, jnp.where(sub == 7, b, 0.0))
         out_rows = lambda a, b: jnp.where(sub < 3, b, jnp.where(sub >= 5, a, 0.0))
         total.append((
-            pos_in[g] + inner + edge_rows(low, high),
+            pos_in[sum_at(g)] + inner + edge_rows(low, high),
             mine_out + outer + edge_rows(s_outer, n_outer),
             mine_rows + out_rows(low, high),
             corner + out_rows(s_outer, n_outer),
         ))
+    for i in oth_edges:
+        wait_recv(i)
+    for q in range(2):
+        for p in range(levels):
+            i = q * levels + p
+            put(ext, (q, 2 * levels - 1 - p), (oth[i],) + ghosts(rowo_in, colo_in, i))
     surface_at = jnp.where(first, 0, 2 * levels - 1)
     for n, (r, l) in enumerate(((0, 0), (0, 128), (8, 0), (8, 128))):
         at = (slice(r, r + 8), slice(l, l + 128))
@@ -530,7 +574,7 @@
     tile = (8, 128)
     vmem = lambda *shape: pltpu.VMEM(shape, f32)
     any_spec = pl.BlockSpec(memory_space=pl.ANY)
-    n_msg = 4 + 2 * CHUNKS + 16
+    n_msg = 4 + 2 * CHUNKS + 24
     big = (2, 2 * levels, 16, 256)
     vmem_spec = pl.BlockSpec(memory_space=pltpu.VMEM)
     results = pl.pallas_call(
@@ -549,8 +593,8 @@
             vmem(2, levels + 1, *tile), vmem(2, levels + 1, *tile),
             vmem(2, *tile), vmem(3, 2, *tile),
             vmem(14, *tile), vmem(14, *tile),
-            vmem(2, levels + 6, *tile), vmem(2, levels + 6, *tile),
-            vmem(3, 2, *tile), vmem(3, 2, *tile),
+            vmem(2, 6, *tile), vmem(2, 6, *tile), vmem(3, 2, *tile), vmem(3, 2, *tile),
+            vmem(2, levels, *tile), vmem(2, levels, *tile), vmem(2, *tile), vmem(3, 2, *tile),
             vmem(dirs, *tile), vmem(4, dirs, *tile), vmem(4, 10, *tile),
             pltpu.SemaphoreType.DMA((7,)),
             pltpu.SemaphoreType.DMA((n_msg,)),

time: 27.3 us -> 27.2 us (level)
  no operation moved by 1% of the time
where the time goes in v5:
time: 27.2 us; the launch traced here: 27.1 us
  Pallas kernels  26.5 us (97%)
  between operations  0.64 us (2%)
    pallas_call x1, Pallas kernels, shards(): pl.pallas_call(functools.partial(kernel, freqs, dirs, levels, lats, lons)...  24.9 us
    pallas_call x1, Pallas kernels, shards(): pl.pallas_call(functools.partial(emit, levels), out_shape=(jax.ShapeDtype...  1.55 us

profile of v5, /device:TPU:1, one launch (start us, length us, event | category | flops | bytes accessed | tf_op | source)
XLA Modules:
  0.0 27.1 jit_solution(15279141525608093786)
XLA Ops:
  0.6 24.9 %window.1 = (f32[5184,128]{1,0:T(8,128)S(1)}, f32[2,8,16,256]{3,2,1,0:T(8,128)S(1)}, f32[3,16,256]{2,1,0:T(8,128)S(1)}, f32[4,16,256]{2,1,0:T(8,128)S(1)}) custom-call(f32[5184,128]{1,0:T(8,128)} %bitcast.2, f32[2,4,8,128]{3,2,1,0:T(8,128)} %cur_hbm.1, s32[8,128]{1,0:T(8,128)} %mask_hbm.1, f32[8,128]{1,0:T(8,128)} %diff_hbm.1, f32[18]{0:T(128)} %courant_hbm.1, ...), custom_call_target="tpu_custom_call" | custom-call | tf_op jit(solution)/shard_map/window/pallas_call | solution.py:580
  25.5 1.5 %emit.1 = (f32[5184,128]{1,0:T(8,128)}, f32[2,4,8,128]{3,2,1,0:T(8,128)}) custom-call(f32[5184,128]{1,0:T(8,128)S(1)} %get-tuple-element.8.spec, f32[2,8,16,256]{3,2,1,0:T(8,128)S(1)} %get-tuple-element.9.ext, f32[3,16,256]{2,1,0:T(8,128)S(1)} %get-tuple-element.10.aux, f32[4,16,256]{2,1,0:T(8,128)S(1)} %get-tuple-element.11.frc), custom_call_target="tpu_custom_call" | custom-call | tf_op jit(solution)/shard_map/emit/pallas_call | solution.py:607

commit v6 on v5

--- a/solution.py
+++ b/solution.py
@@ -32,11 +32,11 @@
 def kernel(
     freqs, dirs, levels, lats, lons,
     spec_hbm, cur_hbm, mask_hbm, diff_hbm, courant_hbm, stokes_hbm, stress_hbm,
-    out_spec, ext, aux, frc,
+    out_spec, ext, aux, gtot, oth, rowo_in, colo_in,
     spec, curv, maskv, diffv, courant, stokes, stress, table,
     send_rows, recv_rows, send_cols, recv_cols,
-    own, oth, edges, rowpk, row_in, colpk, col_in,
-    pos, pos_in, rowc, rowc_in, colc, colc_in, rowo, rowo_in, colo, colo_in,
+    own, edges, rowpk, row_in, colpk, col_in,
+    pos, pos_in, rowc, rowc_in, colc, colc_in, rowo, colo,
     dop, acc, sums,
     local_sem, send_sem, recv_sem,
 ):
@@ -413,26 +413,6 @@
     for i in field_edges:
         wait_recv(i)
 
-    def put(ref, index, quads):
-        for n, (r, l) in enumerate(((0, 0), (0, 128), (8, 0), (8, 128))):
-            ref[index + (slice(r, r + 8), slice(l, l + 128))] = quads[n]
-
-    def ghosts(rows_in, cols_in, i):
-        def lanes(dy):
-            return jnp.where(
-                lane < 4,
-                roll(cols_in[1 + dy, 1], -4 * i, 1),
-                jnp.where(lane >= 124, roll(cols_in[1 + dy, 0], 124 - 4 * i, 1), 0.0),
-            )
-
-        p = i // 2
-        if i % 2 == 0:
-            low, high = roll(rows_in[0, p], 4, 0), rows_in[1, p]
-        else:
-            low, high = rows_in[0, p], roll(rows_in[1, p], 4, 0)
-        corner = jnp.where(sub < 4, lanes(-1), lanes(1))
-        return lanes(0), jnp.where(sub < 4, high, low), corner
-
     for q in range(2):
         for p in range(levels):
             i = q * levels + p
@@ -485,23 +465,40 @@
             mine_rows + out_rows(low, high),
             corner + out_rows(s_outer, n_outer),
         ))
+    for g in range(n_sum):
+        put(gtot, (g,), total[g])
     for i in oth_edges:
         wait_recv(i)
-    for q in range(2):
-        for p in range(levels):
-            i = q * levels + p
-            put(ext, (q, 2 * levels - 1 - p), (oth[i],) + ghosts(rowo_in, colo_in, i))
-    surface_at = jnp.where(first, 0, 2 * levels - 1)
-    for n, (r, l) in enumerate(((0, 0), (0, 128), (8, 0), (8, 128))):
-        at = (slice(r, r + 8), slice(l, l + 128))
-        su = CURRENT_GAIN * ext[(0, surface_at) + at]
-        sv = CURRENT_GAIN * ext[(1, surface_at) + at]
-        for w in range(2):
-            c, s, cc, cs, ss = (total[5 * w + m][n] for m in range(5))
-            frc[(2 * w,) + at] = aux[(0,) + at] * (c + su * cc + sv * cs)
-            frc[(2 * w + 1,) + at] = aux[(0,) + at] * (s + su * cs + sv * ss)
     for i in range(len(messages)):
         wait_send(i)
+
+
+QUADS = ((0, 0), (0, 128), (8, 0), (8, 128))
+
+
+def put(ref, index, quads):
+    for n, (r, l) in enumerate(QUADS):
+        ref[index + (slice(r, r + 8), slice(l, l + 128))] = quads[n]
+
+
+def ghosts(rows_in, cols_in, i):
+    lane = lax.broadcasted_iota(jnp.int32, (8, 128), 1)
+    sub = lax.broadcasted_iota(jnp.int32, (8, 128), 0)
+
+    def lanes(dy):
+        return jnp.where(
+            lane < 4,
+            roll(cols_in[1 + dy, 1], -4 * i, 1),
+            jnp.where(lane >= 124, roll(cols_in[1 + dy, 0], 124 - 4 * i, 1), 0.0),
+        )
+
+    p = i // 2
+    if i % 2 == 0:
+        low, high = roll(rows_in[0, p], 4, 0), rows_in[1, p]
+    else:
+        low, high = rows_in[0, p], roll(rows_in[1, p], 4, 0)
+    corner = jnp.where(sub < 4, lanes(-1), lanes(1))
+    return lanes(0), jnp.where(sub < 4, high, low), corner
 
 
 def level_of(first, total, p):
@@ -542,7 +539,7 @@
             dst[q, own] = (aux[0] * new[q])[0:8, 0:128]
 
 
-def emit(levels, spec, ext, aux, frc, out_spec, out_cur, fa, fb, cur, sems):
+def emit(levels, spec, ext, aux, gtot, oth, rowo, colo, out_spec, out_cur, fa, fb, frc, cur, sems):
     part = spec.shape[0] // EMIT
     copies = []
     for i in range(EMIT):
@@ -552,7 +549,19 @@
         copy.start()
     first = lax.axis_index("sec") == 0
     total = 2 * levels
-    src, dst = ext, fa
+    for q in range(2):
+        for p in range(levels):
+            i = q * levels + p
+            fb[q, p] = ext[q, p]
+            put(fb, (q, total - 1 - p), (oth[i],) + ghosts(rowo, colo, i))
+    surface_at = jnp.where(first, 0, total - 1)
+    su = CURRENT_GAIN * fb[0, surface_at]
+    sv = CURRENT_GAIN * fb[1, surface_at]
+    for w in range(2):
+        c, s, cc, cs, ss = (gtot[5 * w + m] for m in range(5))
+        frc[2 * w] = aux[0] * (c + su * cc + sv * cs)
+        frc[2 * w + 1] = aux[0] * (s + su * cs + sv * ss)
+    src, dst = fb, fa
     for step in range(ITERS):
         for p in range(total - 1 - step):
             ocean_level(src, cur if step == ITERS - 1 else dst, aux, frc, first, total, p)
@@ -579,9 +588,12 @@
     vmem_spec = pl.BlockSpec(memory_space=pltpu.VMEM)
     results = pl.pallas_call(
         functools.partial(kernel, freqs, dirs, levels, lats, lons),
-        out_shape=(vmem(cells, 128), vmem(*big), vmem(3, 16, 256), vmem(4, 16, 256)),
+        out_shape=(
+            vmem(cells, 128), vmem(2, levels, 16, 256), vmem(3, 16, 256), vmem(10, 16, 256),
+            vmem(2 * levels, *tile), vmem(2, levels, *tile), vmem(3, 2, *tile),
+        ),
         in_specs=[any_spec] * 7,
-        out_specs=(vmem_spec,) * 4,
+        out_specs=(vmem_spec,) * 7,
         scratch_shapes=[
             vmem(cells, 128), vmem(2, levels, *tile),
             pltpu.VMEM(tile, jnp.int32), vmem(*tile),
@@ -589,12 +601,12 @@
             pltpu.SMEM((2, dirs), f32),
             vmem(2, CHUNKS, rows, 128), vmem(2, CHUNKS, rows, 128),
             vmem(2, groups, *tile), vmem(2, groups, *tile),
-            vmem(2 * levels, *tile), vmem(2 * levels, *tile), vmem(2, *tile),
+            vmem(2 * levels, *tile), vmem(2, *tile),
             vmem(2, levels + 1, *tile), vmem(2, levels + 1, *tile),
             vmem(2, *tile), vmem(3, 2, *tile),
             vmem(14, *tile), vmem(14, *tile),
             vmem(2, 6, *tile), vmem(2, 6, *tile), vmem(3, 2, *tile), vmem(3, 2, *tile),
-            vmem(2, levels, *tile), vmem(2, levels, *tile), vmem(2, *tile), vmem(3, 2, *tile),
+            vmem(2, levels, *tile), vmem(2, *tile),
             vmem(dirs, *tile), vmem(4, dirs, *tile), vmem(4, 10, *tile),
             pltpu.SemaphoreType.DMA((7,)),
             pltpu.SemaphoreType.DMA((n_msg,)),
@@ -610,10 +622,10 @@
             jax.ShapeDtypeStruct((cells, tile_cols), f32),
             jax.ShapeDtypeStruct(currents.shape, f32),
         ),
-        in_specs=[vmem_spec] * 4,
+        in_specs=[vmem_spec] * 7,
         out_specs=(any_spec, any_spec),
         scratch_shapes=[
-            vmem(*big), vmem(*big), vmem(2, levels, *tile), pltpu.SemaphoreType.DMA((EMIT + 1,)),
+            vmem(*big), vmem(*big), vmem(4, 16, 256), vmem(2, levels, *tile), pltpu.SemaphoreType.DMA((EMIT + 1,)),
         ],
         name="emit",
     )(*results)

time: 27.2 us -> 27.4 us (level)
    pallas_call x1, Pallas kernels: 1.55 us -> 1.85 us  [shards(): pl.pallas_call(functools.partial(emit, levels), out_shape=(jax.ShapeDtype...]
where the time goes in v6:
time: 27.4 us; the launch traced here: 27.3 us
  Pallas kernels  26.6 us (97%)
  between operations  0.64 us (2%)
    pallas_call x1, Pallas kernels, shards(): pl.pallas_call(functools.partial(kernel, freqs, dirs, levels, lats, lons)...  24.8 us
    pallas_call x1, Pallas kernels, shards(): pl.pallas_call(functools.partial(emit, levels), out_shape=(jax.ShapeDtype...  1.85 us

profile of v6, /device:TPU:1, one launch (start us, length us, event | category | flops | bytes accessed | tf_op | source)
XLA Modules:
  0.0 27.3 jit_solution(6877997981296752829)
XLA Ops:
  0.6 24.8 %window.1 = (f32[5184,128]{1,0:T(8,128)S(1)}, f32[2,4,16,256]{3,2,1,0:T(8,128)S(1)}, f32[3,16,256]{2,1,0:T(8,128)S(1)}, f32[10,16,256]{2,1,0:T(8,128)S(1)}, f32[...) custom-call(f32[5184,128]{1,0:T(8,128)} %bitcast.2, f32[2,4,8,128]{3,2,1,0:T(8,128)} %cur_hbm.1, ...), custom_call_target="tpu_custom_call" | custom-call | tf_op jit(solution)/shard_map/window/pallas_call | solution.py:589
  25.4 1.9 %emit.1 = (f32[5184,128]{1,0:T(8,128)}, f32[2,4,8,128]{3,2,1,0:T(8,128)}) custom-call(f32[5184,128]{1,0:T(8,128)S(1)} %get-tuple-element.11.spec, f32[2,4,16,256]{3,2,1,0:T(8,128)S(1)} %get-tuple-element.12.ext, f32[3,16,256]{2,1,0:T(8,128)S(1)} %get-tuple-element.13.aux, f32[10,16,256]{2,1,0:T(8,128)S(1)} %get-tuple-element.14.gtot, ...), custom_call_target="tpu_custom_call" | custom-call | tf_op jit(solution)/shard_map/emit/pallas_call | solution.py:619

commit v7 on v5

--- a/solution.py
+++ b/solution.py
@@ -548,8 +548,8 @@
     for i in range(EMIT):
         at = pl.ds(i * part, part)
         copies.append(pltpu.make_async_copy(spec.at[at], out_spec.at[at], sems.at[i]))
-    for copy in copies:
-        copy.start()
+    for i, copy in enumerate(copies):
+        copy.start(priority=i % 2)
     first = lax.axis_index("sec") == 0
     total = 2 * levels
     src, dst = ext, fa

time: 27.2 us -> 27.2 us (level)
  no operation moved by 1% of the time
where the time goes in v7:
time: 27.2 us; the launch traced here: 27.1 us
  Pallas kernels  26.5 us (97%)
  between operations  0.64 us (2%)
    pallas_call x1, Pallas kernels, shards(): pl.pallas_call(functools.partial(kernel, freqs, dirs, levels, lats, lons)...  24.9 us
    pallas_call x1, Pallas kernels, shards(): pl.pallas_call(functools.partial(emit, levels), out_shape=(jax.ShapeDtype...  1.56 us

profile of v7, /device:TPU:1, one launch (start us, length us, event | category | flops | bytes accessed | tf_op | source)
XLA Modules:
  0.0 27.1 jit_solution(7774747706127103093)
XLA Ops:
  0.6 24.9 %window.1 = (f32[5184,128]{1,0:T(8,128)S(1)}, f32[2,8,16,256]{3,2,1,0:T(8,128)S(1)}, f32[3,16,256]{2,1,0:T(8,128)S(1)}, f32[4,16,256]{2,1,0:T(8,128)S(1)}) custom-call(f32[5184,128]{1,0:T(8,128)} %bitcast.2, f32[2,4,8,128]{3,2,1,0:T(8,128)} %cur_hbm.1, s32[8,128]{1,0:T(8,128)} %mask_hbm.1, f32[8,128]{1,0:T(8,128)} %diff_hbm.1, f32[18]{0:T(128)} %courant_hbm.1, ...), custom_call_target="tpu_custom_call" | custom-call | tf_op jit(solution)/shard_map/window/pallas_call | solution.py:580
  25.5 1.6 %emit.1 = (f32[5184,128]{1,0:T(8,128)}, f32[2,4,8,128]{3,2,1,0:T(8,128)}) custom-call(f32[5184,128]{1,0:T(8,128)S(1)} %get-tuple-element.8.spec, f32[2,8,16,256]{3,2,1,0:T(8,128)S(1)} %get-tuple-element.9.ext, f32[3,16,256]{2,1,0:T(8,128)S(1)} %get-tuple-element.10.aux, f32[4,16,256]{2,1,0:T(8,128)S(1)} %get-tuple-element.11.frc), custom_call_target="tpu_custom_call" | custom-call | tf_op jit(solution)/shard_map/emit/pallas_call | solution.py:607
